TPU v7x, 32 devices: a whole 2x2x4 slice. The times are simulated.
32 devices in a mesh: gx: 4 (over y, x), gy: 8 (over z, core).
Axes of the slice: x: 2, y: 2, z: 4, core: 2. Of those that a mesh axis runs over, the one named last changes fastest.
Arguments:
- basis_fields: float32 [128, 128, 1024], P(None, 'gx', 'gy'), may hold values from -6 to 6
- carried_fields: float32 [128, 128, 1024], P(None, 'gx', 'gy'), may hold values from -70 to 70, as said below
- velocity: float32 [2, 128, 1024], P(None, 'gx', 'gy'), may hold values from -1 to 1
- diffusion: float32 [128, 128], replicated, may hold values from -0.024 to 0.09, as said below
- advection: float32 [128, 128], replicated, may hold values from -0.18 to 0.18
Outputs:
- new_basis: float32 [256, 128, 1024], P(None, 'gx', 'gy')
- galerkin: float32 [256, 128], replicated
Inputs may be any that keep to these rules, and one draw needn't show every extreme that they name: `carried_fields`: entries of the field block are of order one with scales varying over cells and fields. `diffusion`: A positive diagonal with small couplings off it.
All inputs are finite; a program needn't handle non-finite values.
Results may differ from a plain program's by a relative error of at most 0.000086.
Values sent between devices are 32-bit elements; how exact they have to be, the bound alone decides.
No kernel may reach another device: no remote copies, remote signals or barrier semaphores. Data moves between devices by JAX's collectives and lax.ppermute only.
A program may use at most 64 MiB of HBM per device.

v0:
```python
import functools
import jax
import jax.numpy as jnp
from jax import lax
from jax.experimental import pallas as pl
from jax.experimental.pallas import tpu as pltpu
from jax.sharding import PartitionSpec as P


def neighbour(array, axis, step):
    count = lax.axis_size(axis)
    pairs = [(i, (i + step) % count) for i in range(count)]
    return lax.ppermute(array, axis, pairs)


def keep_edges(r, block, top_ref, bottom_ref, first_ref, last_ref, rows, cols):
    if r == 0:
        top_ref[...] = block
    if r == rows - 1:
        bottom_ref[...] = block
    first_ref[:, r:r + 1] = block[:, 0:1]
    last_ref[:, r:r + 1] = block[:, cols - 1:cols]


def edges_kernel(f_ref, top_ref, bottom_ref, first_ref, last_ref, *, count, rows, cols):
    row_lane = lax.broadcasted_iota(jnp.int32, (count, rows), 1)
    firsts = jnp.zeros((count, rows), jnp.float32)
    lasts = jnp.zeros((count, rows), jnp.float32)
    for r in range(rows):
        block = f_ref[pl.ds(r, count, stride=rows), :]
        if r == 0:
            top_ref[...] = block
        if r == rows - 1:
            bottom_ref[...] = block
        firsts = jnp.where(row_lane == r, block[:, 0:1], firsts)
        lasts = jnp.where(row_lane == r, block[:, cols - 1:cols], lasts)
    first_ref[...] = firsts
    last_ref[...] = lasts


def substep_kernel(f_ref, above_ref, below_ref, left_ref, right_ref, vel_ref, mix_ref, out_ref,
                   top_ref, bottom_ref, first_ref, last_ref, *, count, rows, cols):
    col_id = lax.broadcasted_iota(jnp.int32, (count, cols), 1)
    coupling = mix_ref[...]

    def row_of(r):
        if r < 0:
            return above_ref[...]
        if r >= rows:
            return below_ref[...]
        return f_ref[pl.ds(r, count, stride=rows), :]

    prev, here = row_of(-1), row_of(0)
    for r in range(rows):
        nxt = row_of(r + 1)
        west = left_ref[:, r:r + 1]
        east = right_ref[:, r:r + 1]
        minus_y = jnp.where(col_id == 0, west, pltpu.roll(here, 1, 1))
        plus_y = jnp.where(col_id == cols - 1, east, pltpu.roll(here, cols - 1, 1))
        speed_x = vel_ref[r:r + 1, :]
        speed_y = vel_ref[rows + r:rows + r + 1, :]
        laplace = nxt + prev + plus_y + minus_y - 4.0 * here
        transport = speed_x * (nxt - prev) * 0.5 + speed_y * (plus_y - minus_y) * 0.5
        rate = jnp.dot(coupling, jnp.concatenate([laplace, transport], 0),
                       precision=lax.Precision.HIGHEST, preferred_element_type=jnp.float32)
        result = here + rate
        out_ref[pl.ds(r, count, stride=rows), :] = result
        keep_edges(r, result, top_ref, bottom_ref, first_ref, last_ref, rows, cols)
        prev, here = here, nxt


def edge_shapes(count, rows, cols):
    return [
        jax.ShapeDtypeStruct((count, cols), jnp.float32),
        jax.ShapeDtypeStruct((count, cols), jnp.float32),
        jax.ShapeDtypeStruct((count, rows), jnp.float32),
        jax.ShapeDtypeStruct((count, rows), jnp.float32),
    ]


def edges_call(flat, count, rows, cols):
    vmem = pl.BlockSpec(memory_space=pltpu.VMEM)
    return pl.pallas_call(
        functools.partial(edges_kernel, count=count, rows=rows, cols=cols),
        out_shape=edge_shapes(count, rows, cols),
        in_specs=[vmem],
        out_specs=[vmem] * 4,
    )(flat)


def substep_call(flat, above, below, left, right, vel, coupling, count, rows, cols):
    vmem = pl.BlockSpec(memory_space=pltpu.VMEM)
    return pl.pallas_call(
        functools.partial(substep_kernel, count=count, rows=rows, cols=cols),
        out_shape=[jax.ShapeDtypeStruct((count * rows, cols), jnp.float32)]
        + edge_shapes(count, rows, cols),
        in_specs=[vmem] * 7,
        out_specs=[vmem] * 5,
    )(flat, above, below, left, right, vel, coupling)


def one_substep(flat, edges, flat_velocity, coupling, count, rows, cols):
    top, bottom, first, last = edges
    above = neighbour(bottom, "gx", 1)
    below = neighbour(top, "gx", -1)
    left = neighbour(last, "gy", 1)
    right = neighbour(first, "gy", -1)
    result = substep_call(flat, above, below, left, right, flat_velocity, coupling, count, rows, cols)
    return result[0], result[1:]


def exchange_sum(array, axes, last=None):
    stages = []
    for axis in axes:
        count, stride = lax.axis_size(axis), 1
        while stride < count:
            stages.append((axis, stride))
            stride *= 2
    if last in stages:
        stages.remove(last)
        stages.append(last)
    for axis, stride in stages:
        pairs = [(i, i ^ stride) for i in range(lax.axis_size(axis))]
        array = array + lax.ppermute(array, axis, pairs)
    return array


def hdot(a, b):
    return jnp.dot(a, b, precision=lax.Precision.HIGHEST)


def inverse_kernel(a_ref, x_ref, *, size):
    sub = lax.broadcasted_iota(jnp.int32, (size, size), 0)
    lane = lax.broadcasted_iota(jnp.int32, (size, size), 1)
    lane_row = lax.broadcasted_iota(jnp.int32, (1, size), 1)
    sub_col = lax.broadcasted_iota(jnp.int32, (size, 1), 0)

    def row_at(m, k):
        return jnp.sum(jnp.where(sub == k, m, 0.0), axis=0, keepdims=True)

    def col_at(m, k):
        return jnp.sum(jnp.where(lane == k, m, 0.0), axis=1, keepdims=True)

    def lane_at(v, k):
        return jnp.sum(jnp.where(lane_row == k, v, 0.0), axis=1, keepdims=True)

    def step(k, carry):
        a, x, row, col, x_raw = carry
        scale = 1.0 / jnp.sqrt(lane_at(row, k))
        cross = lane_at(row, k + 1) * scale
        low_row = jnp.where(lane_row >= k, row, 0.0) * scale
        low_col = jnp.where(sub_col >= k, col, 0.0) * scale
        x_row = x_raw * scale
        next_row = row_at(a, k + 1) - cross * low_row
        next_col = col_at(a, k + 1) - cross * low_col
        next_x = row_at(x, k + 1) - cross * x_row
        a = a - low_col * low_row
        x = jnp.where(sub == k, x_row, x - jnp.where(sub_col > k, low_col, 0.0) * x_row)
        return a, x, next_row, next_col, next_x

    a0 = a_ref[...]
    eye = jnp.where(sub == lane, 1.0, 0.0).astype(jnp.float32)
    init = (a0, eye, row_at(a0, 0), col_at(a0, 0), row_at(eye, 0))
    x = lax.fori_loop(0, size, step, init, unroll=4)[1]
    x_ref[...] = x


def lower_inverse_call(matrix):
    size = matrix.shape[0]
    vmem = pl.BlockSpec(memory_space=pltpu.VMEM)
    return pl.pallas_call(
        functools.partial(inverse_kernel, size=size),
        out_shape=jax.ShapeDtypeStruct((size, size), jnp.float32),
        in_specs=[vmem],
        out_specs=vmem,
    )(matrix)

def lower_inverse(matrix):
    return lower_inverse_call(0.5 * (matrix + matrix.T))


def body(basis_fields, carried_fields, velocity, diffusion, advection):
    basis_rank, tile_rows, tile_cols = carried_fields.shape
    tile_cells = tile_rows * tile_cols
    aug_count = 2 * basis_rank
    cell_weight = 1.0 / (tile_cells * lax.axis_size("gx") * lax.axis_size("gy"))
    axes = ("gy", "gx")
    flat_basis = basis_fields.reshape(basis_rank, tile_cells)
    flat_carried = carried_fields.reshape(basis_rank, tile_cells)
    known = jnp.concatenate([flat_basis, flat_carried], 0)
    basis_sum = exchange_sum(hdot(flat_basis, known.T), axes) * cell_weight
    flat_velocity = velocity.reshape(2 * tile_rows, tile_cols)
    coupling = jnp.concatenate([diffusion.T, -advection.T], 1)
    shape = (basis_rank, tile_rows, tile_cols)
    carried_rows = carried_fields.reshape(basis_rank * tile_rows, tile_cols)
    edges = edges_call(carried_rows, *shape)
    section_one, edges = one_substep(carried_rows, edges, flat_velocity, coupling, *shape)
    section_two, _ = one_substep(section_one, edges, flat_velocity, coupling, *shape)
    flat_new = section_two.reshape(basis_rank, tile_cells)
    every = jnp.concatenate([flat_basis, flat_new, flat_carried], 0)
    new_sum = exchange_sum(hdot(flat_new, every.T), axes, last=("gy", 1)) * cell_weight
    inverse_11 = lower_inverse(basis_sum[:, :basis_rank])
    low_21 = hdot(new_sum[:, :basis_rank], inverse_11.T)
    schur = new_sum[:, basis_rank:aug_count] - hdot(low_21, low_21.T)
    inverse_22 = lower_inverse(schur)
    top = hdot(inverse_11, flat_basis)
    bottom = hdot(inverse_22, flat_new - hdot(low_21, top))
    new_basis = jnp.concatenate([top, bottom], 0)
    galerkin_top = hdot(inverse_11, basis_sum[:, basis_rank:])
    galerkin_bottom = hdot(inverse_22, new_sum[:, aug_count:] - hdot(low_21, galerkin_top))
    galerkin = jnp.concatenate([galerkin_top, galerkin_bottom], 0)
    return (new_basis.reshape(aug_count, tile_rows, tile_cols), galerkin)


def solution(mesh):
    in_specs = (P(None, "gx", "gy"), P(None, "gx", "gy"), P(None, "gx", "gy"), P(), P())
    out_specs = (P(None, "gx", "gy"), P())
    return jax.shard_map(body, mesh=mesh, in_specs=in_specs, out_specs=out_specs, check_vma=False)
```

profile of v0, /device:TPU:0, one launch (start us, length us, event | category | flops | bytes accessed | tf_op | source)
XLA Modules:
  0.0 134.4 jit_solution(6904921089756922137)
XLA Ops:
  0.6 0.0 copy-start
  0.6 4.3 %shard_map.69 = (f32[128,128]{1,0:T(8,128)}, f32[128,128]{1,0:T(8,128)}, f32[128,32]{1,0:T(8,128)}, f32[128,32]{1,0:T(8,128)}) custom-call(f32[4096,128]{1,0:T(8,128)} %bitcast.41), custom_call_target="tpu_custom_call" | custom-call | tf_op jit(solution)/shard_map/pallas_call | solution.py:83
  4.9 2.9 %collective-permute-start.5 = (f32[128,128]{1,0:T(8,128)}, f32[128,128]{1,0:T(8,128)S(1)}, u32[]{:S(2)}, u32[]{:S(2)}) collective-permute-start(f32[128,128]{1,0:T(8,128)} %get-tuple-element.12), channel_id=1, source_target_pairs={{0,8},{8,16},{16,24},{24,0},{1,9},{9,17},{17,25},{25,1},{2,10},{10... | collective-permute-start | bytes 196616 | tf_op jit(solution)/shard_map/ppermute | solution.py:13
  7.9 1.0 collective-permute-start.6
  8.8 0.0 collective-permute-start.7
  8.8 4.0 %collective-permute-start.8 = (f32[128,32]{1,0:T(8,128)}, f32[128,32]{1,0:T(8,128)S(1)}, u32[]{:S(2)}, u32[]{:S(2)}) collective-permute-start(f32[128,32]{1,0:T(8,128)} %get-tuple-element.15), channel_id=1, source_target_pairs={{0,7},{1,0},{2,1},{3,2},{4,3},{5,4},{6,5},{7,6},{8,15},{9,8},{10,9... | collective-permute-start | bytes 49160 | tf_op jit(solution)/shard_map/ppermute | solution.py:13
  12.9 1.7 %copy.22 = f32[16,8,32,128]{3,1,2,0:T(8,128)S(1)} copy(f32[16,8,32,128]{3,2,1,0:T(8,128)S(1)} %bitcast.43) | data formatting | bytes 4194304
  14.5 1.6 %copy.23 = f32[16,8,32,128]{3,1,2,0:T(8,128)S(1)} copy(f32[16,8,32,128]{3,2,1,0:T(8,128)S(1)} %bitcast.45) | data formatting | bytes 4194304
  16.2 0.0 copy-start.15
  16.2 0.0 copy-start.16
  16.2 3.4 %fusion.10 = f32[128,256]{0,1:T(8,128)S(1)} fusion(f32[128,4096]{1,0:T(8,128)S(1)} %bitcast.48, f32[128,4096]{1,0:T(8,128)S(1)} %bitcast.46), kind=kOutput, calls=%fused_computation.14 | convolution fusion | flops 1611661312 | bytes 4325376 | tf_op jit(solution)/shard_map/dot_general | solution.py:129
  19.7 0.1 collective-permute-start
  19.8 0.1 copy.9
  19.9 0.1 copy.8
  20.0 0.7 pad_maximum_fusion.mix_ref
  20.6 0.0 collective-permute-done.8.right_ref
  20.7 0.0 collective-permute-done.5.above_ref
  20.7 0.6 copy-done.9
  21.3 0.0 copy-done.10
  21.3 0.0 copy-done.7
  21.3 0.0 copy-done.8
  21.4 10.1 %shard_map.70 = (f32[4096,128]{1,0:T(8,128)}, f32[128,128]{1,0:T(8,128)}, f32[128,128]{1,0:T(8,128)}, f32[128,32]{1,0:T(8,128)}, f32[128,32]{1,0:T(8,128)}) custom-call(f32[4096,128]{1,0:T(8,128)} %bitcast.42, f32[128,128]{1,0:T(8,128)} %copy-done.7, f32[128,128]{1,0:T(8,128)} %copy-done.8, f32[128,32]{1,0:T(8,128)} %copy-done.9, f32[128,32]{1,0:T(8,128)} %copy-done.10, ...), custom_call_target="tpu_custom_call" | custom-call | tf_op jit(solution)/shard_map/pallas_call | solution.py:93
  31.4 1.1 collective-permute-start.9
  32.5 1.9 %collective-permute-start.10 = (f32[128,128]{1,0:T(8,128)}, f32[128,128]{1,0:T(8,128)S(1)}, u32[]{:S(2)}, u32[]{:S(2)}) collective-permute-start(f32[128,128]{1,0:T(8,128)} %get-tuple-element.18), channel_id=1, source_target_pairs={{0,24},{8,0},{16,8},{24,16},{1,25},{9,1},{17,9},{25,17},{2,26},{10... | collective-permute-start | bytes 196616 | tf_op jit(solution)/shard_map/ppermute | solution.py:13
  34.3 0.0 collective-permute-start.11
  34.3 3.5 %collective-permute-start.12 = (f32[128,32]{1,0:T(8,128)}, f32[128,32]{1,0:T(8,128)S(1)}, u32[]{:S(2)}, u32[]{:S(2)}) collective-permute-start(f32[128,32]{1,0:T(8,128)} %get-tuple-element.20), channel_id=1, source_target_pairs={{0,7},{1,0},{2,1},{3,2},{4,3},{5,4},{6,5},{7,6},{8,15},{9,8},{10,9... | collective-permute-start | bytes 49160 | tf_op jit(solution)/shard_map/ppermute | solution.py:13
  37.9 2.3 %collective-permute-done.11.left_ref = f32[128,32]{1,0:T(8,128)S(1)} collective-permute-done((f32[128,32]{1,0:T(8,128)}, f32[128,32]{1,0:T(8,128)S(1)}, u32[]{:S(2)}, u32[]{:S(2)}) %collective-permute-start.11) | collective-permute-done | bytes 16416 | tf_op jit(solution)/shard_map/ppermute | solution.py:13
  40.2 0.6 copy-done.13
  40.8 0.0 copy-done.14
  40.8 0.0 copy-done.11
  40.9 10.0 %shard_map.71 = (f32[4096,128]{1,0:T(8,128)}, f32[128,128]{1,0:T(8,128)}, f32[128,128]{1,0:T(8,128)}, f32[128,32]{1,0:T(8,128)}, f32[128,32]{1,0:T(8,128)}) custom-call(f32[4096,128]{1,0:T(8,128)} %get-tuple-element.16.f_ref, f32[128,128]{1,0:T(8,128)} %copy-done.11, f32[128,128]{1,0:T(8,128)} %copy-done.12, f32[128,32]{1,0:T(8,128)} %copy-done.13, ...), custom_call_target="tpu_custom_call" | custom-call | tf_op jit(solution)/shard_map/pallas_call | solution.py:93
  50.8 1.9 %reshape.26 = f32[128,4096]{1,0:T(8,128)S(1)} reshape(f32[4096,128]{1,0:T(8,128)} %get-tuple-element.21) | data formatting | bytes 4194304 | tf_op jit(solution)/shard_map/reshape | solution.py:199
  52.8 0.0 copy-start.1
  52.8 0.1 collective-permute-start.1
  52.9 8.3 %fusion = f32[128,384]{0,1:T(8,128)S(1)} fusion(f32[128,4096]{1,0:T(8,128)S(1)} %reshape.26, f32[128,4096]{1,0:T(8,128)} %bitcast.47, f32[128,4096]{1,0:T(8,128)} %bitcast.49), kind=kOutput, calls=%fused_computation | convolution fusion | flops 2419064832 | bytes 6488064 | tf_op jit(solution)/shard_map/dot_general | solution.py:129
  61.2 1.4 %collective-permute-start.13 = (f32[128,384]{0,1:T(8,128)S(1)}, f32[128,384]{0,1:T(8,128)S(1)}, u32[]{:S(2)}, u32[]{:S(2)}) collective-permute-start(f32[128,384]{0,1:T(8,128)S(1)} %fusion), channel_id=1, source_target_pairs={{0,2},{1,3},{2,0},{3,1},{4,6},{5,7},{6,4},{7,5},{8,10},{9,11},{10,... | collective-permute-start | bytes 589832 | tf_op jit(solution)/shard_map/ppermute | solution.py:124
  62.6 0.1 collective-permute-start.2
  62.7 9.2 %collective-permute-done.2 = f32[128,256]{0,1:T(8,128)S(1)} collective-permute-done((f32[128,256]{0,1:T(8,128)S(1)}, f32[128,256]{0,1:T(8,128)S(1)}, u32[]{:S(2)}, u32[]{:S(2)}) %collective-permute-start.2) | collective-permute-done | bytes 131104 | tf_op jit(solution)/shard_map/ppermute | solution.py:124
  71.9 0.1 collective-permute-start.3
  72.0 1.1 collective-permute-start.14
  73.1 3.9 %collective-permute-done.3 = f32[128,256]{0,1:T(8,128)S(1)} collective-permute-done((f32[128,256]{0,1:T(8,128)S(1)}, f32[128,256]{0,1:T(8,128)S(1)}, u32[]{:S(2)}, u32[]{:S(2)}) %collective-permute-start.3) | collective-permute-done | bytes 131104 | tf_op jit(solution)/shard_map/ppermute | solution.py:124
  77.0 2.1 %collective-permute-start.4 = (f32[128,256]{0,1:T(8,128)S(1)}, f32[128,256]{0,1:T(8,128)S(1)}, u32[]{:S(2)}, u32[]{:S(2)}) collective-permute-start(f32[128,256]{0,1:T(8,128)S(1)} %add.39), channel_id=1, source_target_pairs={{0,16},{8,24},{16,0},{24,8},{1,17},{9,25},{17,1},{25,9},{2,18},{10... | collective-permute-start | bytes 393224 | tf_op jit(solution)/shard_map/ppermute | solution.py:124
  79.1 3.5 %collective-permute-done.14 = f32[128,384]{0,1:T(8,128)S(1)} collective-permute-done((f32[128,384]{0,1:T(8,128)S(1)}, f32[128,384]{0,1:T(8,128)S(1)}, u32[]{:S(2)}, u32[]{:S(2)}) %collective-permute-start.14) | collective-permute-done | bytes 196640 | tf_op jit(solution)/shard_map/ppermute | solution.py:124
  82.5 0.7 collective-permute-start.15
  83.3 0.1 copy.7
  83.4 0.6 fusion.19.a_ref
  84.1 15.2 %shard_map.68 = f32[128,128]{1,0:T(8,128)} custom-call(f32[128,128]{1,0:T(8,128)} %fusion.19.a_ref), custom_call_target="tpu_custom_call" | custom-call | tf_op jit(solution)/shard_map/pallas_call | solution.py:171
  99.3 2.0 %collective-permute-start.16 = (f32[128,384]{0,1:T(8,128)S(1)}, f32[128,384]{0,1:T(8,128)S(1)}, u32[]{:S(2)}, u32[]{:S(2)}) collective-permute-start(f32[128,384]{0,1:T(8,128)S(1)} %add.44), channel_id=1, source_target_pairs={{0,16},{8,24},{16,0},{24,8},{1,17},{9,25},{17,1},{25,9},{2,18},{10... | collective-permute-start | bytes 589832 | tf_op jit(solution)/shard_map/ppermute | solution.py:124
  101.3 4.6 %fusion.22 = f32[128,4096]{1,0:T(8,128)S(1)} fusion(f32[128,128]{1,0:T(8,128)} %shard_map.68, f32[16,8,32,128]{3,2,1,0:T(8,128)} %bitcast.44), kind=kOutput, calls=%fused_computation.33 | convolution fusion | flops 805306368 | bytes 4259840 | tf_op jit(solution)/shard_map/dot_general | solution.py:129
  106.0 0.1 collective-permute-start.17
  106.1 0.3 fusion.14
  106.3 1.2 collective-permute-done.17
  107.5 0.3 fusion.16
  107.8 0.3 slice_subtract_fusion.2
  108.1 0.1 copy.13
  108.2 0.6 fusion.18.a_ref
  108.8 15.4 %shard_map.72 = f32[128,128]{1,0:T(8,128)} custom-call(f32[128,128]{1,0:T(8,128)} %fusion.18.a_ref), custom_call_target="tpu_custom_call" | custom-call | tf_op jit(solution)/shard_map/pallas_call | solution.py:171
  124.2 3.6 %convolution_subtract_fusion = f32[128,4096]{1,0:T(8,128)S(1)} fusion(f32[128,4096]{1,0:T(8,128)} %copy-done.1, f32[128,128]{1,0:T(8,128)S(1)} %fusion.16, f32[128,4096]{1,0:T(8,128)S(1)} %fusion.22), kind=kOutput, calls=%fused_computation.6 | convolution fusion | flops 805830656 | bytes 6356992 | tf_op jit(solution)/shard_map/dot_general | solution.py:129
  127.8 1.9 %fusion.23 = f32[128,4096]{1,0:T(8,128)S(1)} fusion(f32[128,128]{1,0:T(8,128)S(1)} %copy-done.6, f32[128,4096]{1,0:T(8,128)S(1)} %convolution_subtract_fusion), kind=kOutput, calls=%fused_computation.34 | convolution fusion | flops 805306368 | bytes 4259840 | tf_op jit(solution)/shard_map/dot_general | solution.py:129
  129.7 0.4 maximum_bitcast_fusion
  130.2 2.8 %copy.18 = f32[32,8,32,128]{3,2,1,0:T(8,128)} copy(f32[32,8,32,128]{3,1,2,0:T(8,128)S(1)} %maximum_bitcast_fusion) | data formatting | bytes 8388608
  132.9 0.3 fusion.24
  133.2 0.3 fusion.13
  133.5 0.7 pad_maximum_fusion.1
  (46 shorter events, 0.3 us)
Async XLA Ops:
  0.6 12.2 %copy-start = (f32[128,32,128]{2,1,0:T(8,128)S(1)}, f32[128,32,128]{2,1,0:T(8,128)}, u32[]{:S(2)}) copy-start(f32[128,32,128]{2,1,0:T(8,128)} %param.6) | copy-start | bytes 6291460
  4.9 15.7 %collective-permute-start.5 = (f32[128,128]{1,0:T(8,128)}, f32[128,128]{1,0:T(8,128)S(1)}, u32[]{:S(2)}, u32[]{:S(2)}) collective-permute-start(f32[128,128]{1,0:T(8,128)} %get-tuple-element.12), channel_id=1, source_target_pairs={{0,8},{8,16},{16,24},{24,0},{1,9},{9,17},{17,25},{25,1},{2,10},{10... | collective-permute-start | bytes 196616 | tf_op jit(solution)/shard_map/ppermute | solution.py:13
  7.9 12.8 %collective-permute-start.6 = (f32[128,128]{1,0:T(8,128)}, f32[128,128]{1,0:T(8,128)S(1)}, u32[]{:S(2)}, u32[]{:S(2)}) collective-permute-start(f32[128,128]{1,0:T(8,128)} %get-tuple-element.13), channel_id=1, source_target_pairs={{0,24},{8,0},{16,8},{24,16},{1,25},{9,1},{17,9},{25,17},{2,26},{10... | collective-permute-start | bytes 196616 | tf_op jit(solution)/shard_map/ppermute | solution.py:13
  8.8 11.8 %collective-permute-start.7 = (f32[128,32]{1,0:T(8,128)}, f32[128,32]{1,0:T(8,128)S(1)}, u32[]{:S(2)}, u32[]{:S(2)}) collective-permute-start(f32[128,32]{1,0:T(8,128)} %get-tuple-element.14), channel_id=1, source_target_pairs={{0,1},{1,2},{2,3},{3,4},{4,5},{5,6},{6,7},{7,0},{8,9},{9,10},{10,1... | collective-permute-start | bytes 49160 | tf_op jit(solution)/shard_map/ppermute | solution.py:13
  8.8 11.8 %collective-permute-start.8 = (f32[128,32]{1,0:T(8,128)}, f32[128,32]{1,0:T(8,128)S(1)}, u32[]{:S(2)}, u32[]{:S(2)}) collective-permute-start(f32[128,32]{1,0:T(8,128)} %get-tuple-element.15), channel_id=1, source_target_pairs={{0,7},{1,0},{2,1},{3,2},{4,3},{5,4},{6,5},{7,6},{8,15},{9,8},{10,9... | collective-permute-start | bytes 49160 | tf_op jit(solution)/shard_map/ppermute | solution.py:13
  12.9 1.7 %copy-start.2 = (f32[128,32,128]{2,1,0:T(8,128)S(1)}, f32[128,32,128]{2,1,0:T(8,128)}, u32[]{:S(2)}) copy-start(f32[128,32,128]{2,1,0:T(8,128)} %param.5) | copy-start | bytes 6291460
  14.5 1.7 %copy-start.3 = (f32[16,8,32,128]{3,1,2,0:T(8,128)}, f32[16,8,32,128]{3,1,2,0:T(8,128)S(1)}, u32[]{:S(2)}) copy-start(f32[16,8,32,128]{3,1,2,0:T(8,128)S(1)} %copy.22) | copy-start | bytes 6291460
  16.2 3.5 %copy-start.4 = (f32[16,8,32,128]{3,1,2,0:T(8,128)}, f32[16,8,32,128]{3,1,2,0:T(8,128)S(1)}, u32[]{:S(2)}) copy-start(f32[16,8,32,128]{3,1,2,0:T(8,128)S(1)} %copy.23) | copy-start | bytes 6291460
  16.2 3.5 %copy-start.15 = (f32[128,128]{1,0:T(8,128)S(1)}, f32[128,128]{1,0:T(8,128)}, u32[]{:S(2)}) copy-start(f32[128,128]{1,0:T(8,128)} %param.9) | copy-start | bytes 196612
  16.2 3.6 %copy-start.16 = (f32[128,128]{1,0:T(8,128)S(1)}, f32[128,128]{1,0:T(8,128)}, u32[]{:S(2)}) copy-start(f32[128,128]{1,0:T(8,128)} %param.8) | copy-start | bytes 196612
  19.7 33.1 %collective-permute-start = (f32[128,256]{0,1:T(8,128)S(1)}, f32[128,256]{0,1:T(8,128)S(1)}, u32[]{:S(2)}, u32[]{:S(2)}) collective-permute-start(f32[128,256]{0,1:T(8,128)S(1)} %fusion.10), channel_id=1, source_target_pairs={{0,1},{1,0},{2,3},{3,2},{4,5},{5,4},{6,7},{7,6},{8,9},{9,8},{10,11... | collective-permute-start | bytes 393224 | tf_op jit(solution)/shard_map/ppermute | solution.py:124
  20.6 0.6 copy-start.9
  20.7 0.6 copy-start.10
  20.7 0.7 copy-start.7
  20.7 0.7 copy-start.8
  31.4 8.7 %collective-permute-start.9 = (f32[128,128]{1,0:T(8,128)}, f32[128,128]{1,0:T(8,128)S(1)}, u32[]{:S(2)}, u32[]{:S(2)}) collective-permute-start(f32[128,128]{1,0:T(8,128)} %get-tuple-element.17), channel_id=1, source_target_pairs={{0,8},{8,16},{16,24},{24,0},{1,9},{9,17},{17,25},{25,1},{2,10},{10... | collective-permute-start | bytes 196616 | tf_op jit(solution)/shard_map/ppermute | solution.py:13
  32.5 7.7 %collective-permute-start.10 = (f32[128,128]{1,0:T(8,128)}, f32[128,128]{1,0:T(8,128)S(1)}, u32[]{:S(2)}, u32[]{:S(2)}) collective-permute-start(f32[128,128]{1,0:T(8,128)} %get-tuple-element.18), channel_id=1, source_target_pairs={{0,24},{8,0},{16,8},{24,16},{1,25},{9,1},{17,9},{25,17},{2,26},{10... | collective-permute-start | bytes 196616 | tf_op jit(solution)/shard_map/ppermute | solution.py:13
  34.3 5.8 %collective-permute-start.11 = (f32[128,32]{1,0:T(8,128)}, f32[128,32]{1,0:T(8,128)S(1)}, u32[]{:S(2)}, u32[]{:S(2)}) collective-permute-start(f32[128,32]{1,0:T(8,128)} %get-tuple-element.19), channel_id=1, source_target_pairs={{0,1},{1,2},{2,3},{3,4},{4,5},{5,6},{6,7},{7,0},{8,9},{9,10},{10,1... | collective-permute-start | bytes 49160 | tf_op jit(solution)/shard_map/ppermute | solution.py:13
  34.3 5.8 %collective-permute-start.12 = (f32[128,32]{1,0:T(8,128)}, f32[128,32]{1,0:T(8,128)S(1)}, u32[]{:S(2)}, u32[]{:S(2)}) collective-permute-start(f32[128,32]{1,0:T(8,128)} %get-tuple-element.20), channel_id=1, source_target_pairs={{0,7},{1,0},{2,1},{3,2},{4,3},{5,4},{6,5},{7,6},{8,15},{9,8},{10,9... | collective-permute-start | bytes 49160 | tf_op jit(solution)/shard_map/ppermute | solution.py:13
  40.2 0.6 copy-start.13
  40.2 0.7 copy-start.14
  40.2 0.7 copy-start.11
  40.2 0.7 copy-start.12
  52.8 8.4 %copy-start.1 = (f32[128,4096]{1,0:T(8,128)}, f32[128,4096]{1,0:T(8,128)S(1)}, u32[]{:S(2)}) copy-start(f32[128,4096]{1,0:T(8,128)S(1)} %reshape.26) | copy-start | bytes 6291460
  52.8 9.8 %collective-permute-start.1 = (f32[128,256]{0,1:T(8,128)S(1)}, f32[128,256]{0,1:T(8,128)S(1)}, u32[]{:S(2)}, u32[]{:S(2)}) collective-permute-start(f32[128,256]{0,1:T(8,128)S(1)} %add.36), channel_id=1, source_target_pairs={{0,2},{1,3},{2,0},{3,1},{4,6},{5,7},{6,4},{7,5},{8,10},{9,11},{10,... | collective-permute-start | bytes 393224 | tf_op jit(solution)/shard_map/ppermute | solution.py:124
  61.2 10.8 %collective-permute-start.13 = (f32[128,384]{0,1:T(8,128)S(1)}, f32[128,384]{0,1:T(8,128)S(1)}, u32[]{:S(2)}, u32[]{:S(2)}) collective-permute-start(f32[128,384]{0,1:T(8,128)S(1)} %fusion), channel_id=1, source_target_pairs={{0,2},{1,3},{2,0},{3,1},{4,6},{5,7},{6,4},{7,5},{8,10},{9,11},{10,... | collective-permute-start | bytes 589832 | tf_op jit(solution)/shard_map/ppermute | solution.py:124
  62.6 9.3 %collective-permute-start.2 = (f32[128,256]{0,1:T(8,128)S(1)}, f32[128,256]{0,1:T(8,128)S(1)}, u32[]{:S(2)}, u32[]{:S(2)}) collective-permute-start(f32[128,256]{0,1:T(8,128)S(1)} %add.37), channel_id=1, source_target_pairs={{0,4},{1,5},{2,6},{3,7},{4,0},{5,1},{6,2},{7,3},{8,12},{9,13},{10,... | collective-permute-start | bytes 393224 | tf_op jit(solution)/shard_map/ppermute | solution.py:124
  71.9 5.0 %collective-permute-start.3 = (f32[128,256]{0,1:T(8,128)S(1)}, f32[128,256]{0,1:T(8,128)S(1)}, u32[]{:S(2)}, u32[]{:S(2)}) collective-permute-start(f32[128,256]{0,1:T(8,128)S(1)} %add.38), channel_id=1, source_target_pairs={{0,8},{8,0},{16,24},{24,16},{1,9},{9,1},{17,25},{25,17},{2,10},{10... | collective-permute-start | bytes 393224 | tf_op jit(solution)/shard_map/ppermute | solution.py:124
  72.0 10.5 %collective-permute-start.14 = (f32[128,384]{0,1:T(8,128)S(1)}, f32[128,384]{0,1:T(8,128)S(1)}, u32[]{:S(2)}, u32[]{:S(2)}) collective-permute-start(f32[128,384]{0,1:T(8,128)S(1)} %add.42), channel_id=1, source_target_pairs={{0,4},{1,5},{2,6},{3,7},{4,0},{5,1},{6,2},{7,3},{8,12},{9,13},{10,... | collective-permute-start | bytes 589832 | tf_op jit(solution)/shard_map/ppermute | solution.py:124
  77.0 6.3 %collective-permute-start.4 = (f32[128,256]{0,1:T(8,128)S(1)}, f32[128,256]{0,1:T(8,128)S(1)}, u32[]{:S(2)}, u32[]{:S(2)}) collective-permute-start(f32[128,256]{0,1:T(8,128)S(1)} %add.39), channel_id=1, source_target_pairs={{0,16},{8,24},{16,0},{24,8},{1,17},{9,25},{17,1},{25,9},{2,18},{10... | collective-permute-start | bytes 393224 | tf_op jit(solution)/shard_map/ppermute | solution.py:124
  82.5 16.7 %collective-permute-start.15 = (f32[128,384]{0,1:T(8,128)S(1)}, f32[128,384]{0,1:T(8,128)S(1)}, u32[]{:S(2)}, u32[]{:S(2)}) collective-permute-start(f32[128,384]{0,1:T(8,128)S(1)} %add.43), channel_id=1, source_target_pairs={{0,8},{8,0},{16,24},{24,16},{1,9},{9,1},{17,25},{25,17},{2,10},{10... | collective-permute-start | bytes 589832 | tf_op jit(solution)/shard_map/ppermute | solution.py:124
  99.3 6.8 %copy-start.5 = (f32[128,128]{1,0:T(8,128)S(1)}, f32[128,128]{1,0:T(8,128)}, u32[]{:S(2)}) copy-start(f32[128,128]{1,0:T(8,128)} %shard_map.68) | copy-start | bytes 196612
  99.3 6.6 %collective-permute-start.16 = (f32[128,384]{0,1:T(8,128)S(1)}, f32[128,384]{0,1:T(8,128)S(1)}, u32[]{:S(2)}, u32[]{:S(2)}) collective-permute-start(f32[128,384]{0,1:T(8,128)S(1)} %add.44), channel_id=1, source_target_pairs={{0,16},{8,24},{16,0},{24,8},{1,17},{9,25},{17,1},{25,9},{2,18},{10... | collective-permute-start | bytes 589832 | tf_op jit(solution)/shard_map/ppermute | solution.py:124
  106.0 1.5 %collective-permute-start.17 = (f32[128,384]{0,1:T(8,128)S(1)}, f32[128,384]{0,1:T(8,128)S(1)}, u32[]{:S(2)}, u32[]{:S(2)}) collective-permute-start(f32[128,384]{0,1:T(8,128)S(1)} %add.45), channel_id=1, source_target_pairs={{0,1},{1,0},{2,3},{3,2},{4,5},{5,4},{6,7},{7,6},{8,9},{9,8},{10,11... | collective-permute-start | bytes 589832 | tf_op jit(solution)/shard_map/ppermute | solution.py:124
  124.2 3.6 %copy-start.6 = (f32[128,128]{1,0:T(8,128)S(1)}, f32[128,128]{1,0:T(8,128)}, u32[]{:S(2)}) copy-start(f32[128,128]{1,0:T(8,128)} %shard_map.72) | copy-start | bytes 196612
where the time goes:
time: 137 us; the launch traced here: 134 us
  Pallas kernels  54.9 us (40%)
  matrix products  23.1 us (17%)
  starting transfers between devices  22.1 us (16%)
  waiting for transfers between devices  20 us (15%)
  local copies, waits for them, and re-layouts  9.72 us (7%)
  other arithmetic  3.24 us (2%)
    pallas_call x2, Pallas kernels, lower_inverse_call(): pl.pallas_call(functools.partial(inverse_kernel, size=size), out_shape=ja...  30.6 us
    dot_general x10, matrix products, hdot(): return jnp.dot(a, b, precision=lax.Precision.HIGHEST)  23.1 us
    pallas_call x2, Pallas kernels, substep_call(): pl.pallas_call(functools.partial(substep_kernel, count=count, rows=rows,...  20 us
    ppermute x10, waiting for transfers between devices, exchange_sum(): array = array + lax.ppermute(array, axis, pairs)  17.7 us
    ppermute x8, starting transfers between devices, neighbour(): return lax.ppermute(array, axis, pairs)  14.4 us
    ppermute x10, starting transfers between devices, exchange_sum(): array = array + lax.ppermute(array, axis, pairs)  7.72 us
    unnamed x39, local copies, waits for them, and re-layouts  7.59 us
    pallas_call x1, Pallas kernels, edges_call(): pl.pallas_call(functools.partial(edges_kernel, count=count, rows=rows, co...  4.28 us
  transfers between devices with their start and end apart: 18, of which 5 were waited for; matrix products, arithmetic and copies ran while one was open for 17% of the time, Pallas kernels for 26%

commit v1 on v0

--- a/solution.py
+++ b/solution.py
@@ -50,6 +50,9 @@
             return below_ref[...]
         return f_ref[pl.ds(r, count, stride=rows), :]
 
+    row_lane = lax.broadcasted_iota(jnp.int32, (count, rows), 1)
+    firsts = jnp.zeros((count, rows), jnp.float32)
+    lasts = jnp.zeros((count, rows), jnp.float32)
     prev, here = row_of(-1), row_of(0)
     for r in range(rows):
         nxt = row_of(r + 1)
@@ -65,8 +68,15 @@
                        precision=lax.Precision.HIGHEST, preferred_element_type=jnp.float32)
         result = here + rate
         out_ref[pl.ds(r, count, stride=rows), :] = result
-        keep_edges(r, result, top_ref, bottom_ref, first_ref, last_ref, rows, cols)
+        if r == 0:
+            top_ref[...] = result
+        if r == rows - 1:
+            bottom_ref[...] = result
+        firsts = jnp.where(row_lane == r, result[:, 0:1], firsts)
+        lasts = jnp.where(row_lane == r, result[:, cols - 1:cols], lasts)
         prev, here = here, nxt
+    first_ref[...] = firsts
+    last_ref[...] = lasts
 
 
 def edge_shapes(count, rows, cols):

time: 137 us -> 138 us (level)
  transfers between devices with their start and end apart: 18 -> 18, of which waited for: 5 -> 5; matrix products, arithmetic and copies ran while one was open for 17% -> 17% of each run, Pallas kernels for 26% -> 27%
where the time goes in v1:
time: 138 us; the launch traced here: 136 us
  Pallas kernels  56.2 us (41%)
  matrix products  23.1 us (17%)
  starting transfers between devices  22.1 us (16%)
  waiting for transfers between devices  20 us (14%)
  local copies, waits for them, and re-layouts  9.72 us (7%)
  other arithmetic  3.24 us (2%)
    pallas_call x2, Pallas kernels, lower_inverse_call(): pl.pallas_call(functools.partial(inverse_kernel, size=size), out_shape=ja...  30.6 us
    dot_general x10, matrix products, hdot(): return jnp.dot(a, b, precision=lax.Precision.HIGHEST)  23.1 us
    pallas_call x2, Pallas kernels, substep_call(): pl.pallas_call(functools.partial(substep_kernel, count=count, rows=rows,...  21.3 us
    ppermute x10, waiting for transfers between devices, exchange_sum(): array = array + lax.ppermute(array, axis, pairs)  17.7 us
    ppermute x8, starting transfers between devices, neighbour(): return lax.ppermute(array, axis, pairs)  14.4 us
    ppermute x10, starting transfers between devices, exchange_sum(): array = array + lax.ppermute(array, axis, pairs)  7.71 us
    unnamed x39, local copies, waits for them, and re-layouts  7.59 us
    pallas_call x1, Pallas kernels, edges_call(): pl.pallas_call(functools.partial(edges_kernel, count=count, rows=rows, co...  4.28 us
  transfers between devices with their start and end apart: 18, of which 5 were waited for; matrix products, arithmetic and copies ran while one was open for 17% of the time, Pallas kernels for 27%

profile of v1, /device:TPU:0, one launch (start us, length us, event | category | flops | bytes accessed | tf_op | source)
XLA Modules:
  0.0 135.7 jit_solution(16576143358434268959)
XLA Ops:
  0.6 0.0 copy-start
  0.6 4.3 %shard_map.69 = (f32[128,128]{1,0:T(8,128)}, f32[128,128]{1,0:T(8,128)}, f32[128,32]{1,0:T(8,128)}, f32[128,32]{1,0:T(8,128)}) custom-call(f32[4096,128]{1,0:T(8,128)} %bitcast.41), custom_call_target="tpu_custom_call" | custom-call | tf_op jit(solution)/shard_map/pallas_call | solution.py:93
  4.9 2.9 %collective-permute-start.5 = (f32[128,128]{1,0:T(8,128)}, f32[128,128]{1,0:T(8,128)S(1)}, u32[]{:S(2)}, u32[]{:S(2)}) collective-permute-start(f32[128,128]{1,0:T(8,128)} %get-tuple-element.12), channel_id=1, source_target_pairs={{0,8},{8,16},{16,24},{24,0},{1,9},{9,17},{17,25},{25,1},{2,10},{10... | collective-permute-start | bytes 196616 | tf_op jit(solution)/shard_map/ppermute | solution.py:13
  7.9 1.0 collective-permute-start.6
  8.8 0.0 collective-permute-start.7
  8.8 4.0 %collective-permute-start.8 = (f32[128,32]{1,0:T(8,128)}, f32[128,32]{1,0:T(8,128)S(1)}, u32[]{:S(2)}, u32[]{:S(2)}) collective-permute-start(f32[128,32]{1,0:T(8,128)} %get-tuple-element.15), channel_id=1, source_target_pairs={{0,7},{1,0},{2,1},{3,2},{4,3},{5,4},{6,5},{7,6},{8,15},{9,8},{10,9... | collective-permute-start | bytes 49160 | tf_op jit(solution)/shard_map/ppermute | solution.py:13
  12.9 1.7 %copy.22 = f32[16,8,32,128]{3,1,2,0:T(8,128)S(1)} copy(f32[16,8,32,128]{3,2,1,0:T(8,128)S(1)} %bitcast.43) | data formatting | bytes 4194304
  14.5 1.6 %copy.23 = f32[16,8,32,128]{3,1,2,0:T(8,128)S(1)} copy(f32[16,8,32,128]{3,2,1,0:T(8,128)S(1)} %bitcast.45) | data formatting | bytes 4194304
  16.2 0.0 copy-start.15
  16.2 0.0 copy-start.16
  16.2 3.4 %fusion.10 = f32[128,256]{0,1:T(8,128)S(1)} fusion(f32[128,4096]{1,0:T(8,128)S(1)} %bitcast.48, f32[128,4096]{1,0:T(8,128)S(1)} %bitcast.46), kind=kOutput, calls=%fused_computation.14 | convolution fusion | flops 1611661312 | bytes 4325376 | tf_op jit(solution)/shard_map/dot_general | solution.py:139
  19.7 0.1 collective-permute-start
  19.8 0.1 copy.9
  19.9 0.1 copy.8
  20.0 0.7 pad_maximum_fusion.mix_ref
  20.6 0.0 collective-permute-done.7.left_ref
  20.6 0.0 collective-permute-done.8.right_ref
  20.7 0.0 collective-permute-done.6.below_ref
  20.7 0.6 copy-done.9
  21.3 0.0 copy-done.10
  21.3 0.0 copy-done.7
  21.3 0.0 copy-done.8
  21.4 10.7 %shard_map.70 = (f32[4096,128]{1,0:T(8,128)}, f32[128,128]{1,0:T(8,128)}, f32[128,128]{1,0:T(8,128)}, f32[128,32]{1,0:T(8,128)}, f32[128,32]{1,0:T(8,128)}) custom-call(f32[4096,128]{1,0:T(8,128)} %bitcast.42, f32[128,128]{1,0:T(8,128)} %copy-done.7, f32[128,128]{1,0:T(8,128)} %copy-done.8, f32[128,32]{1,0:T(8,128)} %copy-done.9, f32[128,32]{1,0:T(8,128)} %copy-done.10, ...), custom_call_target="tpu_custom_call" | custom-call | tf_op jit(solution)/shard_map/pallas_call | solution.py:103
  32.1 1.1 collective-permute-start.9
  33.1 1.9 %collective-permute-start.10 = (f32[128,128]{1,0:T(8,128)}, f32[128,128]{1,0:T(8,128)S(1)}, u32[]{:S(2)}, u32[]{:S(2)}) collective-permute-start(f32[128,128]{1,0:T(8,128)} %get-tuple-element.18), channel_id=1, source_target_pairs={{0,24},{8,0},{16,8},{24,16},{1,25},{9,1},{17,9},{25,17},{2,26},{10... | collective-permute-start | bytes 196616 | tf_op jit(solution)/shard_map/ppermute | solution.py:13
  35.0 3.5 %collective-permute-start.12 = (f32[128,32]{1,0:T(8,128)}, f32[128,32]{1,0:T(8,128)S(1)}, u32[]{:S(2)}, u32[]{:S(2)}) collective-permute-start(f32[128,32]{1,0:T(8,128)} %get-tuple-element.20), channel_id=1, source_target_pairs={{0,7},{1,0},{2,1},{3,2},{4,3},{5,4},{6,5},{7,6},{8,15},{9,8},{10,9... | collective-permute-start | bytes 49160 | tf_op jit(solution)/shard_map/ppermute | solution.py:13
  38.5 2.3 %collective-permute-done.11.left_ref = f32[128,32]{1,0:T(8,128)S(1)} collective-permute-done((f32[128,32]{1,0:T(8,128)}, f32[128,32]{1,0:T(8,128)S(1)}, u32[]{:S(2)}, u32[]{:S(2)}) %collective-permute-start.11) | collective-permute-done | bytes 16416 | tf_op jit(solution)/shard_map/ppermute | solution.py:13
  40.8 0.6 copy-done.13
  41.4 0.0 copy-done.14
  41.5 0.0 copy-done.11
  41.5 10.6 %shard_map.71 = (f32[4096,128]{1,0:T(8,128)}, f32[128,128]{1,0:T(8,128)}, f32[128,128]{1,0:T(8,128)}, f32[128,32]{1,0:T(8,128)}, f32[128,32]{1,0:T(8,128)}) custom-call(f32[4096,128]{1,0:T(8,128)} %get-tuple-element.16.f_ref, f32[128,128]{1,0:T(8,128)} %copy-done.11, f32[128,128]{1,0:T(8,128)} %copy-done.12, f32[128,32]{1,0:T(8,128)} %copy-done.13, ...), custom_call_target="tpu_custom_call" | custom-call | tf_op jit(solution)/shard_map/pallas_call | solution.py:103
  52.1 1.9 %reshape.26 = f32[128,4096]{1,0:T(8,128)S(1)} reshape(f32[4096,128]{1,0:T(8,128)} %get-tuple-element.21) | data formatting | bytes 4194304 | tf_op jit(solution)/shard_map/reshape | solution.py:209
  54.0 0.0 copy-start.1
  54.1 0.1 collective-permute-start.1
  54.2 8.3 %fusion = f32[128,384]{0,1:T(8,128)S(1)} fusion(f32[128,4096]{1,0:T(8,128)S(1)} %reshape.26, f32[128,4096]{1,0:T(8,128)} %bitcast.47, f32[128,4096]{1,0:T(8,128)} %bitcast.49), kind=kOutput, calls=%fused_computation | convolution fusion | flops 2419064832 | bytes 6488064 | tf_op jit(solution)/shard_map/dot_general | solution.py:139
  62.4 1.4 %collective-permute-start.13 = (f32[128,384]{0,1:T(8,128)S(1)}, f32[128,384]{0,1:T(8,128)S(1)}, u32[]{:S(2)}, u32[]{:S(2)}) collective-permute-start(f32[128,384]{0,1:T(8,128)S(1)} %fusion), channel_id=1, source_target_pairs={{0,2},{1,3},{2,0},{3,1},{4,6},{5,7},{6,4},{7,5},{8,10},{9,11},{10,... | collective-permute-start | bytes 589832 | tf_op jit(solution)/shard_map/ppermute | solution.py:134
  63.9 0.1 collective-permute-start.2
  64.0 9.2 %collective-permute-done.2 = f32[128,256]{0,1:T(8,128)S(1)} collective-permute-done((f32[128,256]{0,1:T(8,128)S(1)}, f32[128,256]{0,1:T(8,128)S(1)}, u32[]{:S(2)}, u32[]{:S(2)}) %collective-permute-start.2) | collective-permute-done | bytes 131104 | tf_op jit(solution)/shard_map/ppermute | solution.py:134
  73.2 0.1 collective-permute-start.3
  73.3 1.1 collective-permute-start.14
  74.4 3.9 %collective-permute-done.3 = f32[128,256]{0,1:T(8,128)S(1)} collective-permute-done((f32[128,256]{0,1:T(8,128)S(1)}, f32[128,256]{0,1:T(8,128)S(1)}, u32[]{:S(2)}, u32[]{:S(2)}) %collective-permute-start.3) | collective-permute-done | bytes 131104 | tf_op jit(solution)/shard_map/ppermute | solution.py:134
  78.3 2.1 %collective-permute-start.4 = (f32[128,256]{0,1:T(8,128)S(1)}, f32[128,256]{0,1:T(8,128)S(1)}, u32[]{:S(2)}, u32[]{:S(2)}) collective-permute-start(f32[128,256]{0,1:T(8,128)S(1)} %add.39), channel_id=1, source_target_pairs={{0,16},{8,24},{16,0},{24,8},{1,17},{9,25},{17,1},{25,9},{2,18},{10... | collective-permute-start | bytes 393224 | tf_op jit(solution)/shard_map/ppermute | solution.py:134
  80.3 3.5 %collective-permute-done.14 = f32[128,384]{0,1:T(8,128)S(1)} collective-permute-done((f32[128,384]{0,1:T(8,128)S(1)}, f32[128,384]{0,1:T(8,128)S(1)}, u32[]{:S(2)}, u32[]{:S(2)}) %collective-permute-start.14) | collective-permute-done | bytes 196640 | tf_op jit(solution)/shard_map/ppermute | solution.py:134
  83.8 0.7 collective-permute-start.15
  84.6 0.1 copy.7
  84.7 0.6 fusion.19.a_ref
  85.3 15.2 %shard_map.68 = f32[128,128]{1,0:T(8,128)} custom-call(f32[128,128]{1,0:T(8,128)} %fusion.19.a_ref), custom_call_target="tpu_custom_call" | custom-call | tf_op jit(solution)/shard_map/pallas_call | solution.py:181
  100.6 2.0 %collective-permute-start.16 = (f32[128,384]{0,1:T(8,128)S(1)}, f32[128,384]{0,1:T(8,128)S(1)}, u32[]{:S(2)}, u32[]{:S(2)}) collective-permute-start(f32[128,384]{0,1:T(8,128)S(1)} %add.44), channel_id=1, source_target_pairs={{0,16},{8,24},{16,0},{24,8},{1,17},{9,25},{17,1},{25,9},{2,18},{10... | collective-permute-start | bytes 589832 | tf_op jit(solution)/shard_map/ppermute | solution.py:134
  102.6 4.6 %fusion.22 = f32[128,4096]{1,0:T(8,128)S(1)} fusion(f32[128,128]{1,0:T(8,128)} %shard_map.68, f32[16,8,32,128]{3,2,1,0:T(8,128)} %bitcast.44), kind=kOutput, calls=%fused_computation.33 | convolution fusion | flops 805306368 | bytes 4259840 | tf_op jit(solution)/shard_map/dot_general | solution.py:139
  107.2 0.1 collective-permute-start.17
  107.3 0.3 fusion.14
  107.6 1.2 collective-permute-done.17
  108.8 0.3 fusion.16
  109.1 0.3 slice_subtract_fusion.2
  109.3 0.1 copy.13
  109.4 0.6 fusion.18.a_ref
  110.1 15.4 %shard_map.72 = f32[128,128]{1,0:T(8,128)} custom-call(f32[128,128]{1,0:T(8,128)} %fusion.18.a_ref), custom_call_target="tpu_custom_call" | custom-call | tf_op jit(solution)/shard_map/pallas_call | solution.py:181
  125.5 3.6 %convolution_subtract_fusion = f32[128,4096]{1,0:T(8,128)S(1)} fusion(f32[128,4096]{1,0:T(8,128)} %copy-done.1, f32[128,128]{1,0:T(8,128)S(1)} %fusion.16, f32[128,4096]{1,0:T(8,128)S(1)} %fusion.22), kind=kOutput, calls=%fused_computation.6 | convolution fusion | flops 805830656 | bytes 6356992 | tf_op jit(solution)/shard_map/dot_general | solution.py:139
  129.1 1.9 %fusion.23 = f32[128,4096]{1,0:T(8,128)S(1)} fusion(f32[128,128]{1,0:T(8,128)S(1)} %copy-done.6, f32[128,4096]{1,0:T(8,128)S(1)} %convolution_subtract_fusion), kind=kOutput, calls=%fused_computation.34 | convolution fusion | flops 805306368 | bytes 4259840 | tf_op jit(solution)/shard_map/dot_general | solution.py:139
  131.0 0.4 maximum_bitcast_fusion
  131.4 2.8 %copy.18 = f32[32,8,32,128]{3,2,1,0:T(8,128)} copy(f32[32,8,32,128]{3,1,2,0:T(8,128)S(1)} %maximum_bitcast_fusion) | data formatting | bytes 8388608
  134.2 0.3 fusion.24
  134.5 0.3 fusion.13
  134.8 0.7 pad_maximum_fusion.1
  (46 shorter events, 0.3 us)
Async XLA Ops:
  0.6 12.2 %copy-start = (f32[128,32,128]{2,1,0:T(8,128)S(1)}, f32[128,32,128]{2,1,0:T(8,128)}, u32[]{:S(2)}) copy-start(f32[128,32,128]{2,1,0:T(8,128)} %param.6) | copy-start | bytes 6291460
  4.9 15.7 %collective-permute-start.5 = (f32[128,128]{1,0:T(8,128)}, f32[128,128]{1,0:T(8,128)S(1)}, u32[]{:S(2)}, u32[]{:S(2)}) collective-permute-start(f32[128,128]{1,0:T(8,128)} %get-tuple-element.12), channel_id=1, source_target_pairs={{0,8},{8,16},{16,24},{24,0},{1,9},{9,17},{17,25},{25,1},{2,10},{10... | collective-permute-start | bytes 196616 | tf_op jit(solution)/shard_map/ppermute | solution.py:13
  7.9 12.8 %collective-permute-start.6 = (f32[128,128]{1,0:T(8,128)}, f32[128,128]{1,0:T(8,128)S(1)}, u32[]{:S(2)}, u32[]{:S(2)}) collective-permute-start(f32[128,128]{1,0:T(8,128)} %get-tuple-element.13), channel_id=1, source_target_pairs={{0,24},{8,0},{16,8},{24,16},{1,25},{9,1},{17,9},{25,17},{2,26},{10... | collective-permute-start | bytes 196616 | tf_op jit(solution)/shard_map/ppermute | solution.py:13
  8.8 11.8 %collective-permute-start.7 = (f32[128,32]{1,0:T(8,128)}, f32[128,32]{1,0:T(8,128)S(1)}, u32[]{:S(2)}, u32[]{:S(2)}) collective-permute-start(f32[128,32]{1,0:T(8,128)} %get-tuple-element.14), channel_id=1, source_target_pairs={{0,1},{1,2},{2,3},{3,4},{4,5},{5,6},{6,7},{7,0},{8,9},{9,10},{10,1... | collective-permute-start | bytes 49160 | tf_op jit(solution)/shard_map/ppermute | solution.py:13
  8.8 11.8 %collective-permute-start.8 = (f32[128,32]{1,0:T(8,128)}, f32[128,32]{1,0:T(8,128)S(1)}, u32[]{:S(2)}, u32[]{:S(2)}) collective-permute-start(f32[128,32]{1,0:T(8,128)} %get-tuple-element.15), channel_id=1, source_target_pairs={{0,7},{1,0},{2,1},{3,2},{4,3},{5,4},{6,5},{7,6},{8,15},{9,8},{10,9... | collective-permute-start | bytes 49160 | tf_op jit(solution)/shard_map/ppermute | solution.py:13
  12.9 1.7 %copy-start.2 = (f32[128,32,128]{2,1,0:T(8,128)S(1)}, f32[128,32,128]{2,1,0:T(8,128)}, u32[]{:S(2)}) copy-start(f32[128,32,128]{2,1,0:T(8,128)} %param.5) | copy-start | bytes 6291460
  14.5 1.7 %copy-start.3 = (f32[16,8,32,128]{3,1,2,0:T(8,128)}, f32[16,8,32,128]{3,1,2,0:T(8,128)S(1)}, u32[]{:S(2)}) copy-start(f32[16,8,32,128]{3,1,2,0:T(8,128)S(1)} %copy.22) | copy-start | bytes 6291460
  16.2 3.5 %copy-start.4 = (f32[16,8,32,128]{3,1,2,0:T(8,128)}, f32[16,8,32,128]{3,1,2,0:T(8,128)S(1)}, u32[]{:S(2)}) copy-start(f32[16,8,32,128]{3,1,2,0:T(8,128)S(1)} %copy.23) | copy-start | bytes 6291460
  16.2 3.5 %copy-start.15 = (f32[128,128]{1,0:T(8,128)S(1)}, f32[128,128]{1,0:T(8,128)}, u32[]{:S(2)}) copy-start(f32[128,128]{1,0:T(8,128)} %param.9) | copy-start | bytes 196612
  16.2 3.6 %copy-start.16 = (f32[128,128]{1,0:T(8,128)S(1)}, f32[128,128]{1,0:T(8,128)}, u32[]{:S(2)}) copy-start(f32[128,128]{1,0:T(8,128)} %param.8) | copy-start | bytes 196612
  19.7 34.4 %collective-permute-start = (f32[128,256]{0,1:T(8,128)S(1)}, f32[128,256]{0,1:T(8,128)S(1)}, u32[]{:S(2)}, u32[]{:S(2)}) collective-permute-start(f32[128,256]{0,1:T(8,128)S(1)} %fusion.10), channel_id=1, source_target_pairs={{0,1},{1,0},{2,3},{3,2},{4,5},{5,4},{6,7},{7,6},{8,9},{9,8},{10,11... | collective-permute-start | bytes 393224 | tf_op jit(solution)/shard_map/ppermute | solution.py:134
  20.6 0.6 copy-start.9
  20.7 0.6 copy-start.10
  20.7 0.7 copy-start.7
  20.7 0.7 copy-start.8
  32.1 8.7 %collective-permute-start.9 = (f32[128,128]{1,0:T(8,128)}, f32[128,128]{1,0:T(8,128)S(1)}, u32[]{:S(2)}, u32[]{:S(2)}) collective-permute-start(f32[128,128]{1,0:T(8,128)} %get-tuple-element.17), channel_id=1, source_target_pairs={{0,8},{8,16},{16,24},{24,0},{1,9},{9,17},{17,25},{25,1},{2,10},{10... | collective-permute-start | bytes 196616 | tf_op jit(solution)/shard_map/ppermute | solution.py:13
  33.1 7.7 %collective-permute-start.10 = (f32[128,128]{1,0:T(8,128)}, f32[128,128]{1,0:T(8,128)S(1)}, u32[]{:S(2)}, u32[]{:S(2)}) collective-permute-start(f32[128,128]{1,0:T(8,128)} %get-tuple-element.18), channel_id=1, source_target_pairs={{0,24},{8,0},{16,8},{24,16},{1,25},{9,1},{17,9},{25,17},{2,26},{10... | collective-permute-start | bytes 196616 | tf_op jit(solution)/shard_map/ppermute | solution.py:13
  35.0 5.8 %collective-permute-start.11 = (f32[128,32]{1,0:T(8,128)}, f32[128,32]{1,0:T(8,128)S(1)}, u32[]{:S(2)}, u32[]{:S(2)}) collective-permute-start(f32[128,32]{1,0:T(8,128)} %get-tuple-element.19), channel_id=1, source_target_pairs={{0,1},{1,2},{2,3},{3,4},{4,5},{5,6},{6,7},{7,0},{8,9},{9,10},{10,1... | collective-permute-start | bytes 49160 | tf_op jit(solution)/shard_map/ppermute | solution.py:13
  35.0 5.8 %collective-permute-start.12 = (f32[128,32]{1,0:T(8,128)}, f32[128,32]{1,0:T(8,128)S(1)}, u32[]{:S(2)}, u32[]{:S(2)}) collective-permute-start(f32[128,32]{1,0:T(8,128)} %get-tuple-element.20), channel_id=1, source_target_pairs={{0,7},{1,0},{2,1},{3,2},{4,3},{5,4},{6,5},{7,6},{8,15},{9,8},{10,9... | collective-permute-start | bytes 49160 | tf_op jit(solution)/shard_map/ppermute | solution.py:13
  40.8 0.6 copy-start.13
  40.8 0.7 copy-start.14
  40.8 0.7 copy-start.11
  40.8 0.7 copy-start.12
  54.0 8.4 %copy-start.1 = (f32[128,4096]{1,0:T(8,128)}, f32[128,4096]{1,0:T(8,128)S(1)}, u32[]{:S(2)}) copy-start(f32[128,4096]{1,0:T(8,128)S(1)} %reshape.26) | copy-start | bytes 6291460
  54.1 9.8 %collective-permute-start.1 = (f32[128,256]{0,1:T(8,128)S(1)}, f32[128,256]{0,1:T(8,128)S(1)}, u32[]{:S(2)}, u32[]{:S(2)}) collective-permute-start(f32[128,256]{0,1:T(8,128)S(1)} %add.36), channel_id=1, source_target_pairs={{0,2},{1,3},{2,0},{3,1},{4,6},{5,7},{6,4},{7,5},{8,10},{9,11},{10,... | collective-permute-start | bytes 393224 | tf_op jit(solution)/shard_map/ppermute | solution.py:134
  62.4 10.8 %collective-permute-start.13 = (f32[128,384]{0,1:T(8,128)S(1)}, f32[128,384]{0,1:T(8,128)S(1)}, u32[]{:S(2)}, u32[]{:S(2)}) collective-permute-start(f32[128,384]{0,1:T(8,128)S(1)} %fusion), channel_id=1, source_target_pairs={{0,2},{1,3},{2,0},{3,1},{4,6},{5,7},{6,4},{7,5},{8,10},{9,11},{10,... | collective-permute-start | bytes 589832 | tf_op jit(solution)/shard_map/ppermute | solution.py:134
  63.9 9.3 %collective-permute-start.2 = (f32[128,256]{0,1:T(8,128)S(1)}, f32[128,256]{0,1:T(8,128)S(1)}, u32[]{:S(2)}, u32[]{:S(2)}) collective-permute-start(f32[128,256]{0,1:T(8,128)S(1)} %add.37), channel_id=1, source_target_pairs={{0,4},{1,5},{2,6},{3,7},{4,0},{5,1},{6,2},{7,3},{8,12},{9,13},{10,... | collective-permute-start | bytes 393224 | tf_op jit(solution)/shard_map/ppermute | solution.py:134
  73.2 5.0 %collective-permute-start.3 = (f32[128,256]{0,1:T(8,128)S(1)}, f32[128,256]{0,1:T(8,128)S(1)}, u32[]{:S(2)}, u32[]{:S(2)}) collective-permute-start(f32[128,256]{0,1:T(8,128)S(1)} %add.38), channel_id=1, source_target_pairs={{0,8},{8,0},{16,24},{24,16},{1,9},{9,1},{17,25},{25,17},{2,10},{10... | collective-permute-start | bytes 393224 | tf_op jit(solution)/shard_map/ppermute | solution.py:134
  73.3 10.5 %collective-permute-start.14 = (f32[128,384]{0,1:T(8,128)S(1)}, f32[128,384]{0,1:T(8,128)S(1)}, u32[]{:S(2)}, u32[]{:S(2)}) collective-permute-start(f32[128,384]{0,1:T(8,128)S(1)} %add.42), channel_id=1, source_target_pairs={{0,4},{1,5},{2,6},{3,7},{4,0},{5,1},{6,2},{7,3},{8,12},{9,13},{10,... | collective-permute-start | bytes 589832 | tf_op jit(solution)/shard_map/ppermute | solution.py:134
  78.3 6.3 %collective-permute-start.4 = (f32[128,256]{0,1:T(8,128)S(1)}, f32[128,256]{0,1:T(8,128)S(1)}, u32[]{:S(2)}, u32[]{:S(2)}) collective-permute-start(f32[128,256]{0,1:T(8,128)S(1)} %add.39), channel_id=1, source_target_pairs={{0,16},{8,24},{16,0},{24,8},{1,17},{9,25},{17,1},{25,9},{2,18},{10... | collective-permute-start | bytes 393224 | tf_op jit(solution)/shard_map/ppermute | solution.py:134
  83.8 16.7 %collective-permute-start.15 = (f32[128,384]{0,1:T(8,128)S(1)}, f32[128,384]{0,1:T(8,128)S(1)}, u32[]{:S(2)}, u32[]{:S(2)}) collective-permute-start(f32[128,384]{0,1:T(8,128)S(1)} %add.43), channel_id=1, source_target_pairs={{0,8},{8,0},{16,24},{24,16},{1,9},{9,1},{17,25},{25,17},{2,10},{10... | collective-permute-start | bytes 589832 | tf_op jit(solution)/shard_map/ppermute | solution.py:134
  100.6 6.8 %copy-start.5 = (f32[128,128]{1,0:T(8,128)S(1)}, f32[128,128]{1,0:T(8,128)}, u32[]{:S(2)}) copy-start(f32[128,128]{1,0:T(8,128)} %shard_map.68) | copy-start | bytes 196612
  100.6 6.6 %collective-permute-start.16 = (f32[128,384]{0,1:T(8,128)S(1)}, f32[128,384]{0,1:T(8,128)S(1)}, u32[]{:S(2)}, u32[]{:S(2)}) collective-permute-start(f32[128,384]{0,1:T(8,128)S(1)} %add.44), channel_id=1, source_target_pairs={{0,16},{8,24},{16,0},{24,8},{1,17},{9,25},{17,1},{25,9},{2,18},{10... | collective-permute-start | bytes 589832 | tf_op jit(solution)/shard_map/ppermute | solution.py:134
  107.2 1.5 %collective-permute-start.17 = (f32[128,384]{0,1:T(8,128)S(1)}, f32[128,384]{0,1:T(8,128)S(1)}, u32[]{:S(2)}, u32[]{:S(2)}) collective-permute-start(f32[128,384]{0,1:T(8,128)S(1)} %add.45), channel_id=1, source_target_pairs={{0,1},{1,0},{2,3},{3,2},{4,5},{5,4},{6,7},{7,6},{8,9},{9,8},{10,11... | collective-permute-start | bytes 589832 | tf_op jit(solution)/shard_map/ppermute | solution.py:134
  125.5 3.6 %copy-start.6 = (f32[128,128]{1,0:T(8,128)S(1)}, f32[128,128]{1,0:T(8,128)}, u32[]{:S(2)}) copy-start(f32[128,128]{1,0:T(8,128)} %shard_map.72) | copy-start | bytes 196612

commit v2 on v0

--- a/solution.py
+++ b/solution.py
@@ -109,7 +109,7 @@
     return result[0], result[1:]
 
 
-def exchange_sum(array, axes, last=None):
+def exchange_sum(array, axes, last=None, first=None):
     stages = []
     for axis in axes:
         count, stride = lax.axis_size(axis), 1
@@ -119,6 +119,9 @@
     if last in stages:
         stages.remove(last)
         stages.append(last)
+    if first in stages:
+        stages.remove(first)
+        stages.insert(0, first)
     for axis, stride in stages:
         pairs = [(i, i ^ stride) for i in range(lax.axis_size(axis))]
         array = array + lax.ppermute(array, axis, pairs)
@@ -198,7 +201,7 @@
     section_two, _ = one_substep(section_one, edges, flat_velocity, coupling, *shape)
     flat_new = section_two.reshape(basis_rank, tile_cells)
     every = jnp.concatenate([flat_basis, flat_new, flat_carried], 0)
-    new_sum = exchange_sum(hdot(flat_new, every.T), axes, last=("gy", 1)) * cell_weight
+    new_sum = exchange_sum(hdot(flat_new, every.T), axes, last=("gy", 1), first=("gy", 4)) * cell_weight
     inverse_11 = lower_inverse(basis_sum[:, :basis_rank])
     low_21 = hdot(new_sum[:, :basis_rank], inverse_11.T)
     schur = new_sum[:, basis_rank:aug_count] - hdot(low_21, low_21.T)

time: 137 us -> 144 us (1.051)
  waiting for transfers between devices: 20 us -> 25.2 us
    ppermute x10, waiting for transfers between devices: 17.7 us -> 22.9 us  [exchange_sum(): array = array + lax.ppermute(array, axis, pairs)]
  transfers between devices with their start and end apart: 18 -> 18, of which waited for: 5 -> 5; matrix products, arithmetic and copies ran while one was open for 17% -> 17% of each run, Pallas kernels for 26% -> 25%
where the time goes in v2:
time: 144 us; the launch traced here: 141 us
  Pallas kernels  54.9 us (38%)
  waiting for transfers between devices  25.2 us (18%)
  starting transfers between devices  23.5 us (16%)
  matrix products  23.1 us (16%)
  local copies, waits for them, and re-layouts  9.72 us (7%)
  other arithmetic  3.24 us (2%)
    pallas_call x2, Pallas kernels, lower_inverse_call(): pl.pallas_call(functools.partial(inverse_kernel, size=size), out_shape=ja...  30.6 us
    dot_general x10, matrix products, hdot(): return jnp.dot(a, b, precision=lax.Precision.HIGHEST)  23.1 us
    ppermute x10, waiting for transfers between devices, exchange_sum(): array = array + lax.ppermute(array, axis, pairs)  22.9 us
    pallas_call x2, Pallas kernels, substep_call(): pl.pallas_call(functools.partial(substep_kernel, count=count, rows=rows,...  20 us
    ppermute x8, starting transfers between devices, neighbour(): return lax.ppermute(array, axis, pairs)  14.4 us
    ppermute x10, starting transfers between devices, exchange_sum(): array = array + lax.ppermute(array, axis, pairs)  9.08 us
    unnamed x39, local copies, waits for them, and re-layouts  7.59 us
    pallas_call x1, Pallas kernels, edges_call(): pl.pallas_call(functools.partial(edges_kernel, count=count, rows=rows, co...  4.28 us
  transfers between devices with their start and end apart: 18, of which 5 were waited for; matrix products, arithmetic and copies ran while one was open for 17% of the time, Pallas kernels for 25%

profile of v2, /device:TPU:0, one launch (start us, length us, event | category | flops | bytes accessed | tf_op | source)
XLA Modules:
  0.0 141.0 jit_solution(7472169786462510944)
XLA Ops:
  0.6 0.0 copy-start
  0.6 4.3 %shard_map.69 = (f32[128,128]{1,0:T(8,128)}, f32[128,128]{1,0:T(8,128)}, f32[128,32]{1,0:T(8,128)}, f32[128,32]{1,0:T(8,128)}) custom-call(f32[4096,128]{1,0:T(8,128)} %bitcast.41), custom_call_target="tpu_custom_call" | custom-call | tf_op jit(solution)/shard_map/pallas_call | solution.py:83
  4.9 2.9 %collective-permute-start.5 = (f32[128,128]{1,0:T(8,128)}, f32[128,128]{1,0:T(8,128)S(1)}, u32[]{:S(2)}, u32[]{:S(2)}) collective-permute-start(f32[128,128]{1,0:T(8,128)} %get-tuple-element.12), channel_id=1, source_target_pairs={{0,8},{8,16},{16,24},{24,0},{1,9},{9,17},{17,25},{25,1},{2,10},{10... | collective-permute-start | bytes 196616 | tf_op jit(solution)/shard_map/ppermute | solution.py:13
  7.9 1.0 collective-permute-start.6
  8.8 4.0 %collective-permute-start.8 = (f32[128,32]{1,0:T(8,128)}, f32[128,32]{1,0:T(8,128)S(1)}, u32[]{:S(2)}, u32[]{:S(2)}) collective-permute-start(f32[128,32]{1,0:T(8,128)} %get-tuple-element.15), channel_id=1, source_target_pairs={{0,7},{1,0},{2,1},{3,2},{4,3},{5,4},{6,5},{7,6},{8,15},{9,8},{10,9... | collective-permute-start | bytes 49160 | tf_op jit(solution)/shard_map/ppermute | solution.py:13
  12.9 1.7 %copy.22 = f32[16,8,32,128]{3,1,2,0:T(8,128)S(1)} copy(f32[16,8,32,128]{3,2,1,0:T(8,128)S(1)} %bitcast.43) | data formatting | bytes 4194304
  14.5 1.6 %copy.23 = f32[16,8,32,128]{3,1,2,0:T(8,128)S(1)} copy(f32[16,8,32,128]{3,2,1,0:T(8,128)S(1)} %bitcast.45) | data formatting | bytes 4194304
  16.2 0.0 copy-start.15
  16.2 0.0 copy-start.16
  16.2 3.4 %fusion.10 = f32[128,256]{0,1:T(8,128)S(1)} fusion(f32[128,4096]{1,0:T(8,128)S(1)} %bitcast.48, f32[128,4096]{1,0:T(8,128)S(1)} %bitcast.46), kind=kOutput, calls=%fused_computation.14 | convolution fusion | flops 1611661312 | bytes 4325376 | tf_op jit(solution)/shard_map/dot_general | solution.py:132
  19.7 0.1 collective-permute-start
  19.8 0.1 copy.9
  19.9 0.1 copy.8
  20.0 0.7 pad_maximum_fusion.mix_ref
  20.7 0.0 collective-permute-done.5.above_ref
  20.7 0.6 copy-done.9
  21.3 0.0 copy-done.10
  21.3 0.0 copy-done.7
  21.3 0.0 copy-done.8
  21.4 10.1 %shard_map.70 = (f32[4096,128]{1,0:T(8,128)}, f32[128,128]{1,0:T(8,128)}, f32[128,128]{1,0:T(8,128)}, f32[128,32]{1,0:T(8,128)}, f32[128,32]{1,0:T(8,128)}) custom-call(f32[4096,128]{1,0:T(8,128)} %bitcast.42, f32[128,128]{1,0:T(8,128)} %copy-done.7, f32[128,128]{1,0:T(8,128)} %copy-done.8, f32[128,32]{1,0:T(8,128)} %copy-done.9, f32[128,32]{1,0:T(8,128)} %copy-done.10, ...), custom_call_target="tpu_custom_call" | custom-call | tf_op jit(solution)/shard_map/pallas_call | solution.py:93
  31.4 1.1 collective-permute-start.9
  32.5 1.9 %collective-permute-start.10 = (f32[128,128]{1,0:T(8,128)}, f32[128,128]{1,0:T(8,128)S(1)}, u32[]{:S(2)}, u32[]{:S(2)}) collective-permute-start(f32[128,128]{1,0:T(8,128)} %get-tuple-element.18), channel_id=1, source_target_pairs={{0,24},{8,0},{16,8},{24,16},{1,25},{9,1},{17,9},{25,17},{2,26},{10... | collective-permute-start | bytes 196616 | tf_op jit(solution)/shard_map/ppermute | solution.py:13
  34.3 0.0 collective-permute-start.11
  34.3 3.5 %collective-permute-start.12 = (f32[128,32]{1,0:T(8,128)}, f32[128,32]{1,0:T(8,128)S(1)}, u32[]{:S(2)}, u32[]{:S(2)}) collective-permute-start(f32[128,32]{1,0:T(8,128)} %get-tuple-element.20), channel_id=1, source_target_pairs={{0,7},{1,0},{2,1},{3,2},{4,3},{5,4},{6,5},{7,6},{8,15},{9,8},{10,9... | collective-permute-start | bytes 49160 | tf_op jit(solution)/shard_map/ppermute | solution.py:13
  37.9 2.3 %collective-permute-done.11.left_ref = f32[128,32]{1,0:T(8,128)S(1)} collective-permute-done((f32[128,32]{1,0:T(8,128)}, f32[128,32]{1,0:T(8,128)S(1)}, u32[]{:S(2)}, u32[]{:S(2)}) %collective-permute-start.11) | collective-permute-done | bytes 16416 | tf_op jit(solution)/shard_map/ppermute | solution.py:13
  40.2 0.6 copy-done.13
  40.8 0.0 copy-done.14
  40.8 0.0 copy-done.11
  40.9 10.0 %shard_map.71 = (f32[4096,128]{1,0:T(8,128)}, f32[128,128]{1,0:T(8,128)}, f32[128,128]{1,0:T(8,128)}, f32[128,32]{1,0:T(8,128)}, f32[128,32]{1,0:T(8,128)}) custom-call(f32[4096,128]{1,0:T(8,128)} %get-tuple-element.16.f_ref, f32[128,128]{1,0:T(8,128)} %copy-done.11, f32[128,128]{1,0:T(8,128)} %copy-done.12, f32[128,32]{1,0:T(8,128)} %copy-done.13, ...), custom_call_target="tpu_custom_call" | custom-call | tf_op jit(solution)/shard_map/pallas_call | solution.py:93
  50.8 1.9 %reshape.26 = f32[128,4096]{1,0:T(8,128)S(1)} reshape(f32[4096,128]{1,0:T(8,128)} %get-tuple-element.21) | data formatting | bytes 4194304 | tf_op jit(solution)/shard_map/reshape | solution.py:202
  52.8 0.0 copy-start.1
  52.8 0.0 collective-permute-done
  52.8 0.1 collective-permute-start.1
  52.9 8.3 %fusion = f32[128,384]{0,1:T(8,128)S(1)} fusion(f32[128,4096]{1,0:T(8,128)S(1)} %reshape.26, f32[128,4096]{1,0:T(8,128)} %bitcast.47, f32[128,4096]{1,0:T(8,128)} %bitcast.49), kind=kOutput, calls=%fused_computation | convolution fusion | flops 2419064832 | bytes 6488064 | tf_op jit(solution)/shard_map/dot_general | solution.py:132
  61.2 0.5 collective-permute-start.13
  61.7 2.6 %collective-permute-start.2 = (f32[128,256]{0,1:T(8,128)S(1)}, f32[128,256]{0,1:T(8,128)S(1)}, u32[]{:S(2)}, u32[]{:S(2)}) collective-permute-start(f32[128,256]{0,1:T(8,128)S(1)} %add.37), channel_id=1, source_target_pairs={{0,4},{1,5},{2,6},{3,7},{4,0},{5,1},{6,2},{7,3},{8,12},{9,13},{10,... | collective-permute-start | bytes 393224 | tf_op jit(solution)/shard_map/ppermute | solution.py:127
  64.2 15.3 %collective-permute-done.2 = f32[128,256]{0,1:T(8,128)S(1)} collective-permute-done((f32[128,256]{0,1:T(8,128)S(1)}, f32[128,256]{0,1:T(8,128)S(1)}, u32[]{:S(2)}, u32[]{:S(2)}) %collective-permute-start.2) | collective-permute-done | bytes 131104 | tf_op jit(solution)/shard_map/ppermute | solution.py:127
  79.6 0.6 collective-permute-start.3
  80.2 0.0 collective-permute-done.13
  80.2 0.1 collective-permute-start.14
  80.3 4.7 %collective-permute-done.3 = f32[128,256]{0,1:T(8,128)S(1)} collective-permute-done((f32[128,256]{0,1:T(8,128)S(1)}, f32[128,256]{0,1:T(8,128)S(1)}, u32[]{:S(2)}, u32[]{:S(2)}) %collective-permute-start.3) | collective-permute-done | bytes 131104 | tf_op jit(solution)/shard_map/ppermute | solution.py:127
  85.0 1.9 %collective-permute-start.4 = (f32[128,256]{0,1:T(8,128)S(1)}, f32[128,256]{0,1:T(8,128)S(1)}, u32[]{:S(2)}, u32[]{:S(2)}) collective-permute-start(f32[128,256]{0,1:T(8,128)S(1)} %add.39), channel_id=1, source_target_pairs={{0,16},{8,24},{16,0},{24,8},{1,17},{9,25},{17,1},{25,9},{2,18},{10... | collective-permute-start | bytes 393224 | tf_op jit(solution)/shard_map/ppermute | solution.py:127
  86.9 1.4 %collective-permute-start.15 = (f32[128,384]{0,1:T(8,128)S(1)}, f32[128,384]{0,1:T(8,128)S(1)}, u32[]{:S(2)}, u32[]{:S(2)}) collective-permute-start(f32[128,384]{0,1:T(8,128)S(1)} %add.43), channel_id=1, source_target_pairs={{0,8},{8,0},{16,24},{24,16},{1,9},{9,1},{17,25},{25,17},{2,10},{10... | collective-permute-start | bytes 589832 | tf_op jit(solution)/shard_map/ppermute | solution.py:127
  88.3 1.7 %collective-permute-done.4 = f32[128,256]{0,1:T(8,128)S(1)} collective-permute-done((f32[128,256]{0,1:T(8,128)S(1)}, f32[128,256]{0,1:T(8,128)S(1)}, u32[]{:S(2)}, u32[]{:S(2)}) %collective-permute-start.4) | collective-permute-done | bytes 131104 | tf_op jit(solution)/shard_map/ppermute | solution.py:127
  90.1 0.1 copy.7
  90.2 0.6 fusion.19.a_ref
  90.8 15.2 %shard_map.68 = f32[128,128]{1,0:T(8,128)} custom-call(f32[128,128]{1,0:T(8,128)} %fusion.19.a_ref), custom_call_target="tpu_custom_call" | custom-call | tf_op jit(solution)/shard_map/pallas_call | solution.py:174
  106.0 1.9 %collective-permute-start.16 = (f32[128,384]{0,1:T(8,128)S(1)}, f32[128,384]{0,1:T(8,128)S(1)}, u32[]{:S(2)}, u32[]{:S(2)}) collective-permute-start(f32[128,384]{0,1:T(8,128)S(1)} %add.44), channel_id=1, source_target_pairs={{0,16},{8,24},{16,0},{24,8},{1,17},{9,25},{17,1},{25,9},{2,18},{10... | collective-permute-start | bytes 589832 | tf_op jit(solution)/shard_map/ppermute | solution.py:127
  107.9 4.6 %fusion.22 = f32[128,4096]{1,0:T(8,128)S(1)} fusion(f32[128,128]{1,0:T(8,128)} %shard_map.68, f32[16,8,32,128]{3,2,1,0:T(8,128)} %bitcast.44), kind=kOutput, calls=%fused_computation.33 | convolution fusion | flops 805306368 | bytes 4259840 | tf_op jit(solution)/shard_map/dot_general | solution.py:132
  112.5 0.1 collective-permute-start.17
  112.6 0.3 fusion.14
  112.9 1.2 collective-permute-done.17
  114.1 0.3 fusion.16
  114.4 0.3 slice_subtract_fusion.2
  114.6 0.1 copy.13
  114.7 0.6 fusion.18.a_ref
  115.4 15.4 %shard_map.72 = f32[128,128]{1,0:T(8,128)} custom-call(f32[128,128]{1,0:T(8,128)} %fusion.18.a_ref), custom_call_target="tpu_custom_call" | custom-call | tf_op jit(solution)/shard_map/pallas_call | solution.py:174
  130.8 3.6 %convolution_subtract_fusion = f32[128,4096]{1,0:T(8,128)S(1)} fusion(f32[128,4096]{1,0:T(8,128)} %copy-done.1, f32[128,128]{1,0:T(8,128)S(1)} %fusion.16, f32[128,4096]{1,0:T(8,128)S(1)} %fusion.22), kind=kOutput, calls=%fused_computation.6 | convolution fusion | flops 805830656 | bytes 6356992 | tf_op jit(solution)/shard_map/dot_general | solution.py:132
  134.4 1.9 %fusion.23 = f32[128,4096]{1,0:T(8,128)S(1)} fusion(f32[128,128]{1,0:T(8,128)S(1)} %copy-done.6, f32[128,4096]{1,0:T(8,128)S(1)} %convolution_subtract_fusion), kind=kOutput, calls=%fused_computation.34 | convolution fusion | flops 805306368 | bytes 4259840 | tf_op jit(solution)/shard_map/dot_general | solution.py:132
  136.3 0.4 maximum_bitcast_fusion
  136.7 2.8 %copy.18 = f32[32,8,32,128]{3,2,1,0:T(8,128)} copy(f32[32,8,32,128]{3,1,2,0:T(8,128)S(1)} %maximum_bitcast_fusion) | data formatting | bytes 8388608
  139.5 0.3 fusion.24
  139.8 0.3 fusion.13
  140.1 0.7 pad_maximum_fusion.1
  (46 shorter events, 0.3 us)
Async XLA Ops:
  0.6 12.2 %copy-start = (f32[128,32,128]{2,1,0:T(8,128)S(1)}, f32[128,32,128]{2,1,0:T(8,128)}, u32[]{:S(2)}) copy-start(f32[128,32,128]{2,1,0:T(8,128)} %param.6) | copy-start | bytes 6291460
  4.9 15.7 %collective-permute-start.5 = (f32[128,128]{1,0:T(8,128)}, f32[128,128]{1,0:T(8,128)S(1)}, u32[]{:S(2)}, u32[]{:S(2)}) collective-permute-start(f32[128,128]{1,0:T(8,128)} %get-tuple-element.12), channel_id=1, source_target_pairs={{0,8},{8,16},{16,24},{24,0},{1,9},{9,17},{17,25},{25,1},{2,10},{10... | collective-permute-start | bytes 196616 | tf_op jit(solution)/shard_map/ppermute | solution.py:13
  7.9 12.8 %collective-permute-start.6 = (f32[128,128]{1,0:T(8,128)}, f32[128,128]{1,0:T(8,128)S(1)}, u32[]{:S(2)}, u32[]{:S(2)}) collective-permute-start(f32[128,128]{1,0:T(8,128)} %get-tuple-element.13), channel_id=1, source_target_pairs={{0,24},{8,0},{16,8},{24,16},{1,25},{9,1},{17,9},{25,17},{2,26},{10... | collective-permute-start | bytes 196616 | tf_op jit(solution)/shard_map/ppermute | solution.py:13
  8.8 11.8 %collective-permute-start.7 = (f32[128,32]{1,0:T(8,128)}, f32[128,32]{1,0:T(8,128)S(1)}, u32[]{:S(2)}, u32[]{:S(2)}) collective-permute-start(f32[128,32]{1,0:T(8,128)} %get-tuple-element.14), channel_id=1, source_target_pairs={{0,1},{1,2},{2,3},{3,4},{4,5},{5,6},{6,7},{7,0},{8,9},{9,10},{10,1... | collective-permute-start | bytes 49160 | tf_op jit(solution)/shard_map/ppermute | solution.py:13
  8.8 11.8 %collective-permute-start.8 = (f32[128,32]{1,0:T(8,128)}, f32[128,32]{1,0:T(8,128)S(1)}, u32[]{:S(2)}, u32[]{:S(2)}) collective-permute-start(f32[128,32]{1,0:T(8,128)} %get-tuple-element.15), channel_id=1, source_target_pairs={{0,7},{1,0},{2,1},{3,2},{4,3},{5,4},{6,5},{7,6},{8,15},{9,8},{10,9... | collective-permute-start | bytes 49160 | tf_op jit(solution)/shard_map/ppermute | solution.py:13
  12.9 1.7 %copy-start.2 = (f32[128,32,128]{2,1,0:T(8,128)S(1)}, f32[128,32,128]{2,1,0:T(8,128)}, u32[]{:S(2)}) copy-start(f32[128,32,128]{2,1,0:T(8,128)} %param.5) | copy-start | bytes 6291460
  14.5 1.7 %copy-start.3 = (f32[16,8,32,128]{3,1,2,0:T(8,128)}, f32[16,8,32,128]{3,1,2,0:T(8,128)S(1)}, u32[]{:S(2)}) copy-start(f32[16,8,32,128]{3,1,2,0:T(8,128)S(1)} %copy.22) | copy-start | bytes 6291460
  16.2 3.5 %copy-start.4 = (f32[16,8,32,128]{3,1,2,0:T(8,128)}, f32[16,8,32,128]{3,1,2,0:T(8,128)S(1)}, u32[]{:S(2)}) copy-start(f32[16,8,32,128]{3,1,2,0:T(8,128)S(1)} %copy.23) | copy-start | bytes 6291460
  16.2 3.5 %copy-start.15 = (f32[128,128]{1,0:T(8,128)S(1)}, f32[128,128]{1,0:T(8,128)}, u32[]{:S(2)}) copy-start(f32[128,128]{1,0:T(8,128)} %param.9) | copy-start | bytes 196612
  16.2 3.6 %copy-start.16 = (f32[128,128]{1,0:T(8,128)S(1)}, f32[128,128]{1,0:T(8,128)}, u32[]{:S(2)}) copy-start(f32[128,128]{1,0:T(8,128)} %param.8) | copy-start | bytes 196612
  19.7 33.1 %collective-permute-start = (f32[128,256]{0,1:T(8,128)S(1)}, f32[128,256]{0,1:T(8,128)S(1)}, u32[]{:S(2)}, u32[]{:S(2)}) collective-permute-start(f32[128,256]{0,1:T(8,128)S(1)} %fusion.10), channel_id=1, source_target_pairs={{0,1},{1,0},{2,3},{3,2},{4,5},{5,4},{6,7},{7,6},{8,9},{9,8},{10,11... | collective-permute-start | bytes 393224 | tf_op jit(solution)/shard_map/ppermute | solution.py:127
  20.6 0.6 copy-start.9
  20.7 0.6 copy-start.10
  20.7 0.7 copy-start.7
  20.7 0.7 copy-start.8
  31.4 8.7 %collective-permute-start.9 = (f32[128,128]{1,0:T(8,128)}, f32[128,128]{1,0:T(8,128)S(1)}, u32[]{:S(2)}, u32[]{:S(2)}) collective-permute-start(f32[128,128]{1,0:T(8,128)} %get-tuple-element.17), channel_id=1, source_target_pairs={{0,8},{8,16},{16,24},{24,0},{1,9},{9,17},{17,25},{25,1},{2,10},{10... | collective-permute-start | bytes 196616 | tf_op jit(solution)/shard_map/ppermute | solution.py:13
  32.5 7.7 %collective-permute-start.10 = (f32[128,128]{1,0:T(8,128)}, f32[128,128]{1,0:T(8,128)S(1)}, u32[]{:S(2)}, u32[]{:S(2)}) collective-permute-start(f32[128,128]{1,0:T(8,128)} %get-tuple-element.18), channel_id=1, source_target_pairs={{0,24},{8,0},{16,8},{24,16},{1,25},{9,1},{17,9},{25,17},{2,26},{10... | collective-permute-start | bytes 196616 | tf_op jit(solution)/shard_map/ppermute | solution.py:13
  34.3 5.8 %collective-permute-start.11 = (f32[128,32]{1,0:T(8,128)}, f32[128,32]{1,0:T(8,128)S(1)}, u32[]{:S(2)}, u32[]{:S(2)}) collective-permute-start(f32[128,32]{1,0:T(8,128)} %get-tuple-element.19), channel_id=1, source_target_pairs={{0,1},{1,2},{2,3},{3,4},{4,5},{5,6},{6,7},{7,0},{8,9},{9,10},{10,1... | collective-permute-start | bytes 49160 | tf_op jit(solution)/shard_map/ppermute | solution.py:13
  34.3 5.8 %collective-permute-start.12 = (f32[128,32]{1,0:T(8,128)}, f32[128,32]{1,0:T(8,128)S(1)}, u32[]{:S(2)}, u32[]{:S(2)}) collective-permute-start(f32[128,32]{1,0:T(8,128)} %get-tuple-element.20), channel_id=1, source_target_pairs={{0,7},{1,0},{2,1},{3,2},{4,3},{5,4},{6,5},{7,6},{8,15},{9,8},{10,9... | collective-permute-start | bytes 49160 | tf_op jit(solution)/shard_map/ppermute | solution.py:13
  40.2 0.6 copy-start.13
  40.2 0.7 copy-start.14
  40.2 0.7 copy-start.11
  40.2 0.7 copy-start.12
  52.8 8.4 %copy-start.1 = (f32[128,4096]{1,0:T(8,128)}, f32[128,4096]{1,0:T(8,128)S(1)}, u32[]{:S(2)}) copy-start(f32[128,4096]{1,0:T(8,128)S(1)} %reshape.26) | copy-start | bytes 6291460
  52.8 8.9 %collective-permute-start.1 = (f32[128,256]{0,1:T(8,128)S(1)}, f32[128,256]{0,1:T(8,128)S(1)}, u32[]{:S(2)}, u32[]{:S(2)}) collective-permute-start(f32[128,256]{0,1:T(8,128)S(1)} %add.36), channel_id=1, source_target_pairs={{0,2},{1,3},{2,0},{3,1},{4,6},{5,7},{6,4},{7,5},{8,10},{9,11},{10,... | collective-permute-start | bytes 393224 | tf_op jit(solution)/shard_map/ppermute | solution.py:127
  61.2 19.0 %collective-permute-start.13 = (f32[128,384]{0,1:T(8,128)S(1)}, f32[128,384]{0,1:T(8,128)S(1)}, u32[]{:S(2)}, u32[]{:S(2)}) collective-permute-start(f32[128,384]{0,1:T(8,128)S(1)} %fusion), channel_id=1, source_target_pairs={{0,4},{1,5},{2,6},{3,7},{4,0},{5,1},{6,2},{7,3},{8,12},{9,13},{10,... | collective-permute-start | bytes 589832 | tf_op jit(solution)/shard_map/ppermute | solution.py:127
  61.7 17.9 %collective-permute-start.2 = (f32[128,256]{0,1:T(8,128)S(1)}, f32[128,256]{0,1:T(8,128)S(1)}, u32[]{:S(2)}, u32[]{:S(2)}) collective-permute-start(f32[128,256]{0,1:T(8,128)S(1)} %add.37), channel_id=1, source_target_pairs={{0,4},{1,5},{2,6},{3,7},{4,0},{5,1},{6,2},{7,3},{8,12},{9,13},{10,... | collective-permute-start | bytes 393224 | tf_op jit(solution)/shard_map/ppermute | solution.py:127
  79.6 5.4 %collective-permute-start.3 = (f32[128,256]{0,1:T(8,128)S(1)}, f32[128,256]{0,1:T(8,128)S(1)}, u32[]{:S(2)}, u32[]{:S(2)}) collective-permute-start(f32[128,256]{0,1:T(8,128)S(1)} %add.38), channel_id=1, source_target_pairs={{0,8},{8,0},{16,24},{24,16},{1,9},{9,1},{17,25},{25,17},{2,10},{10... | collective-permute-start | bytes 393224 | tf_op jit(solution)/shard_map/ppermute | solution.py:127
  80.2 6.7 %collective-permute-start.14 = (f32[128,384]{0,1:T(8,128)S(1)}, f32[128,384]{0,1:T(8,128)S(1)}, u32[]{:S(2)}, u32[]{:S(2)}) collective-permute-start(f32[128,384]{0,1:T(8,128)S(1)} %add.42), channel_id=1, source_target_pairs={{0,2},{1,3},{2,0},{3,1},{4,6},{5,7},{6,4},{7,5},{8,10},{9,11},{10,... | collective-permute-start | bytes 589832 | tf_op jit(solution)/shard_map/ppermute | solution.py:127
  85.0 5.0 %collective-permute-start.4 = (f32[128,256]{0,1:T(8,128)S(1)}, f32[128,256]{0,1:T(8,128)S(1)}, u32[]{:S(2)}, u32[]{:S(2)}) collective-permute-start(f32[128,256]{0,1:T(8,128)S(1)} %add.39), channel_id=1, source_target_pairs={{0,16},{8,24},{16,0},{24,8},{1,17},{9,25},{17,1},{25,9},{2,18},{10... | collective-permute-start | bytes 393224 | tf_op jit(solution)/shard_map/ppermute | solution.py:127
  86.9 19.1 %collective-permute-start.15 = (f32[128,384]{0,1:T(8,128)S(1)}, f32[128,384]{0,1:T(8,128)S(1)}, u32[]{:S(2)}, u32[]{:S(2)}) collective-permute-start(f32[128,384]{0,1:T(8,128)S(1)} %add.43), channel_id=1, source_target_pairs={{0,8},{8,0},{16,24},{24,16},{1,9},{9,1},{17,25},{25,17},{2,10},{10... | collective-permute-start | bytes 589832 | tf_op jit(solution)/shard_map/ppermute | solution.py:127
  106.0 6.6 %copy-start.5 = (f32[128,128]{1,0:T(8,128)S(1)}, f32[128,128]{1,0:T(8,128)}, u32[]{:S(2)}) copy-start(f32[128,128]{1,0:T(8,128)} %shard_map.68) | copy-start | bytes 196612
  106.0 6.5 %collective-permute-start.16 = (f32[128,384]{0,1:T(8,128)S(1)}, f32[128,384]{0,1:T(8,128)S(1)}, u32[]{:S(2)}, u32[]{:S(2)}) collective-permute-start(f32[128,384]{0,1:T(8,128)S(1)} %add.44), channel_id=1, source_target_pairs={{0,16},{8,24},{16,0},{24,8},{1,17},{9,25},{17,1},{25,9},{2,18},{10... | collective-permute-start | bytes 589832 | tf_op jit(solution)/shard_map/ppermute | solution.py:127
  112.5 1.5 %collective-permute-start.17 = (f32[128,384]{0,1:T(8,128)S(1)}, f32[128,384]{0,1:T(8,128)S(1)}, u32[]{:S(2)}, u32[]{:S(2)}) collective-permute-start(f32[128,384]{0,1:T(8,128)S(1)} %add.45), channel_id=1, source_target_pairs={{0,1},{1,0},{2,3},{3,2},{4,5},{5,4},{6,7},{7,6},{8,9},{9,8},{10,11... | collective-permute-start | bytes 589832 | tf_op jit(solution)/shard_map/ppermute | solution.py:127
  130.8 3.6 %copy-start.6 = (f32[128,128]{1,0:T(8,128)S(1)}, f32[128,128]{1,0:T(8,128)}, u32[]{:S(2)}) copy-start(f32[128,128]{1,0:T(8,128)} %shard_map.72) | copy-start | bytes 196612

commit v3 on v0

--- a/solution.py
+++ b/solution.py
@@ -109,7 +109,7 @@
     return result[0], result[1:]
 
 
-def exchange_sum(array, axes, last=None):
+def exchange_sum(array, axes, last=None, hold=None):
     stages = []
     for axis in axes:
         count, stride = lax.axis_size(axis), 1
@@ -119,10 +119,12 @@
     if last in stages:
         stages.remove(last)
         stages.append(last)
-    for axis, stride in stages:
+    for number, (axis, stride) in enumerate(stages):
+        if number == len(stages) - 1 and hold is not None:
+            array, hold = lax.optimization_barrier((array, hold))
         pairs = [(i, i ^ stride) for i in range(lax.axis_size(axis))]
         array = array + lax.ppermute(array, axis, pairs)
-    return array
+    return array if hold is None else (array, hold)
 
 
 def hdot(a, b):
@@ -198,8 +200,11 @@
     section_two, _ = one_substep(section_one, edges, flat_velocity, coupling, *shape)
     flat_new = section_two.reshape(basis_rank, tile_cells)
     every = jnp.concatenate([flat_basis, flat_new, flat_carried], 0)
-    new_sum = exchange_sum(hdot(flat_new, every.T), axes, last=("gy", 1)) * cell_weight
     inverse_11 = lower_inverse(basis_sum[:, :basis_rank])
+    new_sum, inverse_11 = exchange_sum(
+        hdot(flat_new, every.T), axes, last=("gy", 1), hold=inverse_11
+    )
+    new_sum = new_sum * cell_weight
     low_21 = hdot(new_sum[:, :basis_rank], inverse_11.T)
     schur = new_sum[:, basis_rank:aug_count] - hdot(low_21, low_21.T)
     inverse_22 = lower_inverse(schur)

time: 137 us -> 140 us (1.022)
  waiting for transfers between devices: 20 us -> 23.7 us
    ppermute x10, waiting for transfers between devices: 17.7 us -> 21.4 us  [exchange_sum(): array = array + lax.ppermute(array, axis, pairs)]
where the time goes in v3:
time: 140 us; the launch traced here: 137 us
  Pallas kernels  54.9 us (39%)
  waiting for transfers between devices  23.7 us (17%)
  matrix products  23.1 us (16%)
  starting transfers between devices  21.1 us (15%)
  local copies, waits for them, and re-layouts  9.72 us (7%)
  other arithmetic  3.23 us (2%)
    pallas_call x2, Pallas kernels, lower_inverse_call(): pl.pallas_call(functools.partial(inverse_kernel, size=size), out_shape=ja...  30.6 us
    dot_general x10, matrix products, hdot(): return jnp.dot(a, b, precision=lax.Precision.HIGHEST)  23.1 us
    ppermute x10, waiting for transfers between devices, exchange_sum(): array = array + lax.ppermute(array, axis, pairs)  21.4 us
    pallas_call x2, Pallas kernels, substep_call(): pl.pallas_call(functools.partial(substep_kernel, count=count, rows=rows,...  20 us
    ppermute x8, starting transfers between devices, neighbour(): return lax.ppermute(array, axis, pairs)  14.4 us
    unnamed x39, local copies, waits for them, and re-layouts  7.59 us
    ppermute x10, starting transfers between devices, exchange_sum(): array = array + lax.ppermute(array, axis, pairs)  6.64 us
    pallas_call x1, Pallas kernels, edges_call(): pl.pallas_call(functools.partial(edges_kernel, count=count, rows=rows, co...  4.28 us
  transfers between devices with their start and end apart: 18, of which 5 were waited for; matrix products, arithmetic and copies ran while one was open for 17% of the time, Pallas kernels for 26%

profile of v3, /device:TPU:0, one launch (start us, length us, event | category | flops | bytes accessed | tf_op | source)
XLA Modules:
  0.0 137.0 jit_solution(5510353901853488503)
XLA Ops:
  0.6 0.0 copy-start
  0.6 4.3 %shard_map.68 = (f32[128,128]{1,0:T(8,128)}, f32[128,128]{1,0:T(8,128)}, f32[128,32]{1,0:T(8,128)}, f32[128,32]{1,0:T(8,128)}) custom-call(f32[4096,128]{1,0:T(8,128)} %bitcast.41), custom_call_target="tpu_custom_call" | custom-call | tf_op jit(solution)/shard_map/pallas_call | solution.py:83
  4.9 2.9 %collective-permute-start = (f32[128,128]{1,0:T(8,128)}, f32[128,128]{1,0:T(8,128)S(1)}, u32[]{:S(2)}, u32[]{:S(2)}) collective-permute-start(f32[128,128]{1,0:T(8,128)} %get-tuple-element.14), channel_id=1, source_target_pairs={{0,8},{8,16},{16,24},{24,0},{1,9},{9,17},{17,25},{25,1},{2,10},{10... | collective-permute-start | bytes 196616 | tf_op jit(solution)/shard_map/ppermute | solution.py:13
  7.9 1.0 collective-permute-start.1
  8.8 0.0 collective-permute-start.2
  8.8 4.0 %collective-permute-start.3 = (f32[128,32]{1,0:T(8,128)}, f32[128,32]{1,0:T(8,128)S(1)}, u32[]{:S(2)}, u32[]{:S(2)}) collective-permute-start(f32[128,32]{1,0:T(8,128)} %get-tuple-element.17), channel_id=1, source_target_pairs={{0,7},{1,0},{2,1},{3,2},{4,3},{5,4},{6,5},{7,6},{8,15},{9,8},{10,9... | collective-permute-start | bytes 49160 | tf_op jit(solution)/shard_map/ppermute | solution.py:13
  12.9 1.7 %copy.22 = f32[16,8,32,128]{3,1,2,0:T(8,128)S(1)} copy(f32[16,8,32,128]{3,2,1,0:T(8,128)S(1)} %bitcast.43) | data formatting | bytes 4194304
  14.5 1.6 %copy.23 = f32[16,8,32,128]{3,1,2,0:T(8,128)S(1)} copy(f32[16,8,32,128]{3,2,1,0:T(8,128)S(1)} %bitcast.45) | data formatting | bytes 4194304
  16.2 0.0 copy-start.15
  16.2 0.0 copy-start.16
  16.2 3.4 %fusion.10 = f32[128,256]{0,1:T(8,128)S(1)} fusion(f32[128,4096]{1,0:T(8,128)S(1)} %bitcast.48, f32[128,4096]{1,0:T(8,128)S(1)} %bitcast.46), kind=kOutput, calls=%fused_computation.14 | convolution fusion | flops 1611661312 | bytes 4325376 | tf_op jit(solution)/shard_map/dot_general | solution.py:131
  19.7 0.1 collective-permute-start.12
  19.8 0.1 copy.8
  19.9 0.1 copy.7
  20.0 0.7 pad_maximum_fusion.mix_ref
  20.6 0.0 collective-permute-done.2.left_ref
  20.6 0.0 collective-permute-done.3.right_ref
  20.7 0.0 collective-permute-done.1.below_ref
  20.7 0.6 copy-done.9
  21.3 0.0 copy-done.10
  21.3 0.0 copy-done.7
  21.3 0.0 copy-done.8
  21.4 10.1 %shard_map.69 = (f32[4096,128]{1,0:T(8,128)}, f32[128,128]{1,0:T(8,128)}, f32[128,128]{1,0:T(8,128)}, f32[128,32]{1,0:T(8,128)}, f32[128,32]{1,0:T(8,128)}) custom-call(f32[4096,128]{1,0:T(8,128)} %bitcast.42, f32[128,128]{1,0:T(8,128)} %copy-done.7, f32[128,128]{1,0:T(8,128)} %copy-done.8, f32[128,32]{1,0:T(8,128)} %copy-done.9, f32[128,32]{1,0:T(8,128)} %copy-done.10, ...), custom_call_target="tpu_custom_call" | custom-call | tf_op jit(solution)/shard_map/pallas_call | solution.py:93
  31.4 1.1 collective-permute-start.4
  32.5 1.9 %collective-permute-start.5 = (f32[128,128]{1,0:T(8,128)}, f32[128,128]{1,0:T(8,128)S(1)}, u32[]{:S(2)}, u32[]{:S(2)}) collective-permute-start(f32[128,128]{1,0:T(8,128)} %get-tuple-element.20), channel_id=1, source_target_pairs={{0,24},{8,0},{16,8},{24,16},{1,25},{9,1},{17,9},{25,17},{2,26},{10... | collective-permute-start | bytes 196616 | tf_op jit(solution)/shard_map/ppermute | solution.py:13
  34.3 3.5 %collective-permute-start.7 = (f32[128,32]{1,0:T(8,128)}, f32[128,32]{1,0:T(8,128)S(1)}, u32[]{:S(2)}, u32[]{:S(2)}) collective-permute-start(f32[128,32]{1,0:T(8,128)} %get-tuple-element.22), channel_id=1, source_target_pairs={{0,7},{1,0},{2,1},{3,2},{4,3},{5,4},{6,5},{7,6},{8,15},{9,8},{10,9... | collective-permute-start | bytes 49160 | tf_op jit(solution)/shard_map/ppermute | solution.py:13
  37.9 2.3 %collective-permute-done.6.left_ref = f32[128,32]{1,0:T(8,128)S(1)} collective-permute-done((f32[128,32]{1,0:T(8,128)}, f32[128,32]{1,0:T(8,128)S(1)}, u32[]{:S(2)}, u32[]{:S(2)}) %collective-permute-start.6) | collective-permute-done | bytes 16416 | tf_op jit(solution)/shard_map/ppermute | solution.py:13
  40.2 0.6 copy-done.13
  40.8 0.0 copy-done.14
  40.8 0.0 copy-done.11
  40.9 10.0 %shard_map.70 = (f32[4096,128]{1,0:T(8,128)}, f32[128,128]{1,0:T(8,128)}, f32[128,128]{1,0:T(8,128)}, f32[128,32]{1,0:T(8,128)}, f32[128,32]{1,0:T(8,128)}) custom-call(f32[4096,128]{1,0:T(8,128)} %get-tuple-element.18.f_ref, f32[128,128]{1,0:T(8,128)} %copy-done.11, f32[128,128]{1,0:T(8,128)} %copy-done.12, f32[128,32]{1,0:T(8,128)} %copy-done.13, ...), custom_call_target="tpu_custom_call" | custom-call | tf_op jit(solution)/shard_map/pallas_call | solution.py:93
  50.8 1.9 %reshape.24 = f32[128,4096]{1,0:T(8,128)S(1)} reshape(f32[4096,128]{1,0:T(8,128)} %get-tuple-element.23) | data formatting | bytes 4194304 | tf_op jit(solution)/shard_map/reshape | solution.py:201
  52.8 0.0 copy-start.1
  52.8 0.1 collective-permute-start.13
  52.9 8.3 %fusion = f32[128,384]{0,1:T(8,128)S(1)} fusion(f32[128,4096]{1,0:T(8,128)S(1)} %reshape.24, f32[128,4096]{1,0:T(8,128)} %bitcast.47, f32[128,4096]{1,0:T(8,128)} %bitcast.49), kind=kOutput, calls=%fused_computation | convolution fusion | flops 2419064832 | bytes 6488064 | tf_op jit(solution)/shard_map/dot_general | solution.py:131
  61.2 1.4 %collective-permute-start.8 = (f32[128,384]{0,1:T(8,128)S(1)}, f32[128,384]{0,1:T(8,128)S(1)}, u32[]{:S(2)}, u32[]{:S(2)}) collective-permute-start(f32[128,384]{0,1:T(8,128)S(1)} %fusion), channel_id=1, source_target_pairs={{0,2},{1,3},{2,0},{3,1},{4,6},{5,7},{6,4},{7,5},{8,10},{9,11},{10,... | collective-permute-start | bytes 589832 | tf_op jit(solution)/shard_map/ppermute | solution.py:126
  62.6 0.1 collective-permute-start.14
  62.7 9.2 %collective-permute-done.14 = f32[128,256]{0,1:T(8,128)S(1)} collective-permute-done((f32[128,256]{0,1:T(8,128)S(1)}, f32[128,256]{0,1:T(8,128)S(1)}, u32[]{:S(2)}, u32[]{:S(2)}) %collective-permute-start.14) | collective-permute-done | bytes 131104 | tf_op jit(solution)/shard_map/ppermute | solution.py:126
  71.9 0.1 collective-permute-start.15
  72.0 1.1 collective-permute-start.9
  73.1 3.9 %collective-permute-done.15 = f32[128,256]{0,1:T(8,128)S(1)} collective-permute-done((f32[128,256]{0,1:T(8,128)S(1)}, f32[128,256]{0,1:T(8,128)S(1)}, u32[]{:S(2)}, u32[]{:S(2)}) %collective-permute-start.15) | collective-permute-done | bytes 131104 | tf_op jit(solution)/shard_map/ppermute | solution.py:126
  77.0 2.1 %collective-permute-start.16 = (f32[128,256]{0,1:T(8,128)S(1)}, f32[128,256]{0,1:T(8,128)S(1)}, u32[]{:S(2)}, u32[]{:S(2)}) collective-permute-start(f32[128,256]{0,1:T(8,128)S(1)} %add.43), channel_id=1, source_target_pairs={{0,16},{8,24},{16,0},{24,8},{1,17},{9,25},{17,1},{25,9},{2,18},{10... | collective-permute-start | bytes 393224 | tf_op jit(solution)/shard_map/ppermute | solution.py:126
  79.1 3.5 %collective-permute-done.9 = f32[128,384]{0,1:T(8,128)S(1)} collective-permute-done((f32[128,384]{0,1:T(8,128)S(1)}, f32[128,384]{0,1:T(8,128)S(1)}, u32[]{:S(2)}, u32[]{:S(2)}) %collective-permute-start.9) | collective-permute-done | bytes 196640 | tf_op jit(solution)/shard_map/ppermute | solution.py:126
  82.5 0.7 collective-permute-start.10
  83.3 0.1 copy.11
  83.4 4.9 %collective-permute-done.10 = f32[128,384]{0,1:T(8,128)S(1)} collective-permute-done((f32[128,384]{0,1:T(8,128)S(1)}, f32[128,384]{0,1:T(8,128)S(1)}, u32[]{:S(2)}, u32[]{:S(2)}) %collective-permute-start.10) | collective-permute-done | bytes 196640 | tf_op jit(solution)/shard_map/ppermute | solution.py:126
  88.3 1.0 collective-permute-start.11
  89.3 0.6 fusion.19.a_ref
  89.9 15.2 %shard_map.71 = f32[128,128]{1,0:T(8,128)} custom-call(f32[128,128]{1,0:T(8,128)} %fusion.19.a_ref), custom_call_target="tpu_custom_call" | custom-call | tf_op jit(solution)/shard_map/pallas_call | solution.py:173
  105.1 0.1 collective-permute-start.17
  105.2 4.6 %fusion.22 = f32[128,4096]{1,0:T(8,128)S(1)} fusion(f32[128,128]{1,0:T(8,128)} %shard_map.71, f32[16,8,32,128]{3,2,1,0:T(8,128)} %bitcast.44), kind=kOutput, calls=%fused_computation.33 | convolution fusion | flops 805306368 | bytes 4259840 | tf_op jit(solution)/shard_map/dot_general | solution.py:131
  109.8 0.3 fusion.14
  110.1 0.3 fusion.16
  110.4 0.3 slice_subtract_fusion.2
  110.7 0.1 copy.13
  110.8 0.6 fusion.18.a_ref
  111.4 15.4 %shard_map.72 = f32[128,128]{1,0:T(8,128)} custom-call(f32[128,128]{1,0:T(8,128)} %fusion.18.a_ref), custom_call_target="tpu_custom_call" | custom-call | tf_op jit(solution)/shard_map/pallas_call | solution.py:173
  126.9 3.6 %convolution_subtract_fusion = f32[128,4096]{1,0:T(8,128)S(1)} fusion(f32[128,4096]{1,0:T(8,128)} %copy-done.1, f32[128,128]{1,0:T(8,128)S(1)} %fusion.16, f32[128,4096]{1,0:T(8,128)S(1)} %fusion.22), kind=kOutput, calls=%fused_computation.6 | convolution fusion | flops 805830656 | bytes 6356992 | tf_op jit(solution)/shard_map/dot_general | solution.py:131
  130.5 1.9 %fusion.23 = f32[128,4096]{1,0:T(8,128)S(1)} fusion(f32[128,128]{1,0:T(8,128)S(1)} %copy-done.6, f32[128,4096]{1,0:T(8,128)S(1)} %convolution_subtract_fusion), kind=kOutput, calls=%fused_computation.34 | convolution fusion | flops 805306368 | bytes 4259840 | tf_op jit(solution)/shard_map/dot_general | solution.py:131
  132.4 0.4 maximum_bitcast_fusion
  132.8 2.8 %copy.18 = f32[32,8,32,128]{3,2,1,0:T(8,128)} copy(f32[32,8,32,128]{3,1,2,0:T(8,128)S(1)} %maximum_bitcast_fusion) | data formatting | bytes 8388608
  135.5 0.3 fusion.24
  135.8 0.3 fusion.13
  136.1 0.7 pad_maximum_fusion.1
  (46 shorter events, 0.3 us)
Async XLA Ops:
  0.6 12.2 %copy-start = (f32[128,32,128]{2,1,0:T(8,128)S(1)}, f32[128,32,128]{2,1,0:T(8,128)}, u32[]{:S(2)}) copy-start(f32[128,32,128]{2,1,0:T(8,128)} %param.6) | copy-start | bytes 6291460
  4.9 15.7 %collective-permute-start = (f32[128,128]{1,0:T(8,128)}, f32[128,128]{1,0:T(8,128)S(1)}, u32[]{:S(2)}, u32[]{:S(2)}) collective-permute-start(f32[128,128]{1,0:T(8,128)} %get-tuple-element.14), channel_id=1, source_target_pairs={{0,8},{8,16},{16,24},{24,0},{1,9},{9,17},{17,25},{25,1},{2,10},{10... | collective-permute-start | bytes 196616 | tf_op jit(solution)/shard_map/ppermute | solution.py:13
  7.9 12.8 %collective-permute-start.1 = (f32[128,128]{1,0:T(8,128)}, f32[128,128]{1,0:T(8,128)S(1)}, u32[]{:S(2)}, u32[]{:S(2)}) collective-permute-start(f32[128,128]{1,0:T(8,128)} %get-tuple-element.15), channel_id=1, source_target_pairs={{0,24},{8,0},{16,8},{24,16},{1,25},{9,1},{17,9},{25,17},{2,26},{10... | collective-permute-start | bytes 196616 | tf_op jit(solution)/shard_map/ppermute | solution.py:13
  8.8 11.8 %collective-permute-start.2 = (f32[128,32]{1,0:T(8,128)}, f32[128,32]{1,0:T(8,128)S(1)}, u32[]{:S(2)}, u32[]{:S(2)}) collective-permute-start(f32[128,32]{1,0:T(8,128)} %get-tuple-element.16), channel_id=1, source_target_pairs={{0,1},{1,2},{2,3},{3,4},{4,5},{5,6},{6,7},{7,0},{8,9},{9,10},{10,1... | collective-permute-start | bytes 49160 | tf_op jit(solution)/shard_map/ppermute | solution.py:13
  8.8 11.8 %collective-permute-start.3 = (f32[128,32]{1,0:T(8,128)}, f32[128,32]{1,0:T(8,128)S(1)}, u32[]{:S(2)}, u32[]{:S(2)}) collective-permute-start(f32[128,32]{1,0:T(8,128)} %get-tuple-element.17), channel_id=1, source_target_pairs={{0,7},{1,0},{2,1},{3,2},{4,3},{5,4},{6,5},{7,6},{8,15},{9,8},{10,9... | collective-permute-start | bytes 49160 | tf_op jit(solution)/shard_map/ppermute | solution.py:13
  12.9 1.7 %copy-start.2 = (f32[128,32,128]{2,1,0:T(8,128)S(1)}, f32[128,32,128]{2,1,0:T(8,128)}, u32[]{:S(2)}) copy-start(f32[128,32,128]{2,1,0:T(8,128)} %param.5) | copy-start | bytes 6291460
  14.5 1.7 %copy-start.3 = (f32[16,8,32,128]{3,1,2,0:T(8,128)}, f32[16,8,32,128]{3,1,2,0:T(8,128)S(1)}, u32[]{:S(2)}) copy-start(f32[16,8,32,128]{3,1,2,0:T(8,128)S(1)} %copy.22) | copy-start | bytes 6291460
  16.2 3.5 %copy-start.4 = (f32[16,8,32,128]{3,1,2,0:T(8,128)}, f32[16,8,32,128]{3,1,2,0:T(8,128)S(1)}, u32[]{:S(2)}) copy-start(f32[16,8,32,128]{3,1,2,0:T(8,128)S(1)} %copy.23) | copy-start | bytes 6291460
  16.2 3.5 %copy-start.15 = (f32[128,128]{1,0:T(8,128)S(1)}, f32[128,128]{1,0:T(8,128)}, u32[]{:S(2)}) copy-start(f32[128,128]{1,0:T(8,128)} %param.9) | copy-start | bytes 196612
  16.2 3.6 %copy-start.16 = (f32[128,128]{1,0:T(8,128)S(1)}, f32[128,128]{1,0:T(8,128)}, u32[]{:S(2)}) copy-start(f32[128,128]{1,0:T(8,128)} %param.8) | copy-start | bytes 196612
  19.7 33.1 %collective-permute-start.12 = (f32[128,256]{0,1:T(8,128)S(1)}, f32[128,256]{0,1:T(8,128)S(1)}, u32[]{:S(2)}, u32[]{:S(2)}) collective-permute-start(f32[128,256]{0,1:T(8,128)S(1)} %fusion.10), channel_id=1, source_target_pairs={{0,1},{1,0},{2,3},{3,2},{4,5},{5,4},{6,7},{7,6},{8,9},{9,8},{10,11... | collective-permute-start | bytes 393224 | tf_op jit(solution)/shard_map/ppermute | solution.py:126
  20.6 0.6 copy-start.9
  20.7 0.6 copy-start.10
  20.7 0.7 copy-start.7
  20.7 0.7 copy-start.8
  31.4 8.7 %collective-permute-start.4 = (f32[128,128]{1,0:T(8,128)}, f32[128,128]{1,0:T(8,128)S(1)}, u32[]{:S(2)}, u32[]{:S(2)}) collective-permute-start(f32[128,128]{1,0:T(8,128)} %get-tuple-element.19), channel_id=1, source_target_pairs={{0,8},{8,16},{16,24},{24,0},{1,9},{9,17},{17,25},{25,1},{2,10},{10... | collective-permute-start | bytes 196616 | tf_op jit(solution)/shard_map/ppermute | solution.py:13
  32.5 7.7 %collective-permute-start.5 = (f32[128,128]{1,0:T(8,128)}, f32[128,128]{1,0:T(8,128)S(1)}, u32[]{:S(2)}, u32[]{:S(2)}) collective-permute-start(f32[128,128]{1,0:T(8,128)} %get-tuple-element.20), channel_id=1, source_target_pairs={{0,24},{8,0},{16,8},{24,16},{1,25},{9,1},{17,9},{25,17},{2,26},{10... | collective-permute-start | bytes 196616 | tf_op jit(solution)/shard_map/ppermute | solution.py:13
  34.3 5.8 %collective-permute-start.6 = (f32[128,32]{1,0:T(8,128)}, f32[128,32]{1,0:T(8,128)S(1)}, u32[]{:S(2)}, u32[]{:S(2)}) collective-permute-start(f32[128,32]{1,0:T(8,128)} %get-tuple-element.21), channel_id=1, source_target_pairs={{0,1},{1,2},{2,3},{3,4},{4,5},{5,6},{6,7},{7,0},{8,9},{9,10},{10,1... | collective-permute-start | bytes 49160 | tf_op jit(solution)/shard_map/ppermute | solution.py:13
  34.3 5.8 %collective-permute-start.7 = (f32[128,32]{1,0:T(8,128)}, f32[128,32]{1,0:T(8,128)S(1)}, u32[]{:S(2)}, u32[]{:S(2)}) collective-permute-start(f32[128,32]{1,0:T(8,128)} %get-tuple-element.22), channel_id=1, source_target_pairs={{0,7},{1,0},{2,1},{3,2},{4,3},{5,4},{6,5},{7,6},{8,15},{9,8},{10,9... | collective-permute-start | bytes 49160 | tf_op jit(solution)/shard_map/ppermute | solution.py:13
  40.2 0.6 copy-start.13
  40.2 0.7 copy-start.14
  40.2 0.7 copy-start.11
  40.2 0.7 copy-start.12
  52.8 8.4 %copy-start.1 = (f32[128,4096]{1,0:T(8,128)}, f32[128,4096]{1,0:T(8,128)S(1)}, u32[]{:S(2)}) copy-start(f32[128,4096]{1,0:T(8,128)S(1)} %reshape.24) | copy-start | bytes 6291460
  52.8 9.8 %collective-permute-start.13 = (f32[128,256]{0,1:T(8,128)S(1)}, f32[128,256]{0,1:T(8,128)S(1)}, u32[]{:S(2)}, u32[]{:S(2)}) collective-permute-start(f32[128,256]{0,1:T(8,128)S(1)} %add.40), channel_id=1, source_target_pairs={{0,2},{1,3},{2,0},{3,1},{4,6},{5,7},{6,4},{7,5},{8,10},{9,11},{10,... | collective-permute-start | bytes 393224 | tf_op jit(solution)/shard_map/ppermute | solution.py:126
  61.2 10.8 %collective-permute-start.8 = (f32[128,384]{0,1:T(8,128)S(1)}, f32[128,384]{0,1:T(8,128)S(1)}, u32[]{:S(2)}, u32[]{:S(2)}) collective-permute-start(f32[128,384]{0,1:T(8,128)S(1)} %fusion), channel_id=1, source_target_pairs={{0,2},{1,3},{2,0},{3,1},{4,6},{5,7},{6,4},{7,5},{8,10},{9,11},{10,... | collective-permute-start | bytes 589832 | tf_op jit(solution)/shard_map/ppermute | solution.py:126
  62.6 9.3 %collective-permute-start.14 = (f32[128,256]{0,1:T(8,128)S(1)}, f32[128,256]{0,1:T(8,128)S(1)}, u32[]{:S(2)}, u32[]{:S(2)}) collective-permute-start(f32[128,256]{0,1:T(8,128)S(1)} %add.41), channel_id=1, source_target_pairs={{0,4},{1,5},{2,6},{3,7},{4,0},{5,1},{6,2},{7,3},{8,12},{9,13},{10,... | collective-permute-start | bytes 393224 | tf_op jit(solution)/shard_map/ppermute | solution.py:126
  71.9 5.0 %collective-permute-start.15 = (f32[128,256]{0,1:T(8,128)S(1)}, f32[128,256]{0,1:T(8,128)S(1)}, u32[]{:S(2)}, u32[]{:S(2)}) collective-permute-start(f32[128,256]{0,1:T(8,128)S(1)} %add.42), channel_id=1, source_target_pairs={{0,8},{8,0},{16,24},{24,16},{1,9},{9,1},{17,25},{25,17},{2,10},{10... | collective-permute-start | bytes 393224 | tf_op jit(solution)/shard_map/ppermute | solution.py:126
  72.0 10.5 %collective-permute-start.9 = (f32[128,384]{0,1:T(8,128)S(1)}, f32[128,384]{0,1:T(8,128)S(1)}, u32[]{:S(2)}, u32[]{:S(2)}) collective-permute-start(f32[128,384]{0,1:T(8,128)S(1)} %add.36), channel_id=1, source_target_pairs={{0,4},{1,5},{2,6},{3,7},{4,0},{5,1},{6,2},{7,3},{8,12},{9,13},{10,... | collective-permute-start | bytes 589832 | tf_op jit(solution)/shard_map/ppermute | solution.py:126
  77.0 6.3 %collective-permute-start.16 = (f32[128,256]{0,1:T(8,128)S(1)}, f32[128,256]{0,1:T(8,128)S(1)}, u32[]{:S(2)}, u32[]{:S(2)}) collective-permute-start(f32[128,256]{0,1:T(8,128)S(1)} %add.43), channel_id=1, source_target_pairs={{0,16},{8,24},{16,0},{24,8},{1,17},{9,25},{17,1},{25,9},{2,18},{10... | collective-permute-start | bytes 393224 | tf_op jit(solution)/shard_map/ppermute | solution.py:126
  82.5 5.7 %collective-permute-start.10 = (f32[128,384]{0,1:T(8,128)S(1)}, f32[128,384]{0,1:T(8,128)S(1)}, u32[]{:S(2)}, u32[]{:S(2)}) collective-permute-start(f32[128,384]{0,1:T(8,128)S(1)} %add.37), channel_id=1, source_target_pairs={{0,8},{8,0},{16,24},{24,16},{1,9},{9,1},{17,25},{25,17},{2,10},{10... | collective-permute-start | bytes 589832 | tf_op jit(solution)/shard_map/ppermute | solution.py:126
  88.3 16.8 %collective-permute-start.11 = (f32[128,384]{0,1:T(8,128)S(1)}, f32[128,384]{0,1:T(8,128)S(1)}, u32[]{:S(2)}, u32[]{:S(2)}) collective-permute-start(f32[128,384]{0,1:T(8,128)S(1)} %add.38), channel_id=1, source_target_pairs={{0,16},{8,24},{16,0},{24,8},{1,17},{9,25},{17,1},{25,9},{2,18},{10... | collective-permute-start | bytes 589832 | tf_op jit(solution)/shard_map/ppermute | solution.py:126
  105.1 4.7 %copy-start.5 = (f32[128,128]{1,0:T(8,128)S(1)}, f32[128,128]{1,0:T(8,128)}, u32[]{:S(2)}) copy-start(f32[128,128]{1,0:T(8,128)} %shard_map.71) | copy-start | bytes 196612
  105.1 5.0 %collective-permute-start.17 = (f32[128,384]{0,1:T(8,128)S(1)}, f32[128,384]{0,1:T(8,128)S(1)}, u32[]{:S(2)}, u32[]{:S(2)}) collective-permute-start(f32[128,384]{0,1:T(8,128)S(1)} %add.39), channel_id=1, source_target_pairs={{0,1},{1,0},{2,3},{3,2},{4,5},{5,4},{6,7},{7,6},{8,9},{9,8},{10,11... | collective-permute-start | bytes 589832 | tf_op jit(solution)/shard_map/ppermute | solution.py:126
  126.9 3.6 %copy-start.6 = (f32[128,128]{1,0:T(8,128)S(1)}, f32[128,128]{1,0:T(8,128)}, u32[]{:S(2)}) copy-start(f32[128,128]{1,0:T(8,128)} %shard_map.72) | copy-start | bytes 196612
